TPU v7x, 32 devices: a whole 2x2x4 slice. The times are simulated.
32 devices in a mesh: rep: 4 (over y, x), ep: 8 (over z, core).
Axes of the slice: x: 2, y: 2, z: 4, core: 2. Of those that a mesh axis runs over, the one named last changes fastest.
Arguments:
- tokens: bfloat16 [8192, 768], P(('rep', 'ep')), may hold values from -6 to 6
- segment_ids: int32 [4, 2048], P('rep', 'ep'), may hold values from 0 to 3, never falling along the last dimension, each value on 1 to 1024 neighbouring positions
- routes: int32 [8192, 2], P(('rep', 'ep')), may hold values from 0 to 7, all different within a row; in each aligned block of 256 rows (0 to 255, 256 to 511, ...) at most 128 rows name the same one
- norm1_gain: bfloat16 [768], P(('rep', 'ep')), may hold values from 0.5 to 1.5
- w_query: bfloat16 [768, 768], P(('rep', 'ep')), may hold values from -0.3125 to 0.3125
- w_key: bfloat16 [768, 768], P(('rep', 'ep')), may hold values from -0.3125 to 0.3125
- w_value: bfloat16 [768, 768], P(('rep', 'ep')), may hold values from -0.21875 to 0.21875
- w_out: bfloat16 [768, 768], P(('rep', 'ep')), may hold values from -1.25 to 1.25
- norm2_gain: bfloat16 [768], P(('rep', 'ep')), may hold values from 0.5 to 1.5
- w_router: bfloat16 [768, 8], P(('rep', 'ep')), may hold values from -0.15625 to 0.15625
- shared_gate: bfloat16 [768, 2048], P(('rep', 'ep')), may hold values from -0.21875 to 0.21875
- shared_up: bfloat16 [768, 2048], P(('rep', 'ep')), may hold values from -0.21875 to 0.21875
- shared_down: bfloat16 [2048, 768], P(('rep', 'ep')), may hold values from -0.1875 to 0.1875
- expert_gate: bfloat16 [8, 768, 2048], P('ep'), may hold values from -0.21875 to 0.21875
- expert_up: bfloat16 [8, 768, 2048], P('ep'), may hold values from -0.21875 to 0.21875
- expert_down: bfloat16 [8, 2048, 768], P('ep'), may hold values from -1.5 to 1.5
- out_grad: bfloat16 [8192, 768], P(('rep', 'ep')), may hold values from -6 to 6
Outputs:
- layer_out: bfloat16 [8192, 768], P(('rep', 'ep'))
- tokens_grad: float32 [8192, 768], P(('rep', 'ep'))
- norm1_gain_grad: float32 [768], P(('rep', 'ep'))
- w_query_grad: float32 [768, 768], P(('rep', 'ep'))
- w_key_grad: float32 [768, 768], P(('rep', 'ep'))
- w_value_grad: float32 [768, 768], P(('rep', 'ep'))
- w_out_grad: float32 [768, 768], P(('rep', 'ep'))
- norm2_gain_grad: float32 [768], P(('rep', 'ep'))
- w_router_grad: float32 [768, 8], P(('rep', 'ep'))
- shared_gate_grad: float32 [768, 2048], P(('rep', 'ep'))
- shared_up_grad: float32 [768, 2048], P(('rep', 'ep'))
- shared_down_grad: float32 [2048, 768], P(('rep', 'ep'))
- expert_gate_grad: float32 [8, 768, 2048], P('ep', None, 'rep')
- expert_up_grad: float32 [8, 768, 2048], P('ep', None, 'rep')
- expert_down_grad: float32 [8, 2048, 768], P('ep', None, 'rep')
Inputs may be any that keep to these rules, and one draw needn't show every extreme that they name: `segment_ids`: along each pack of 2048 places the document number never falls; every document has 1 to 1024 places, and one has exactly 1024. `routes`: each token names 2 different experts. Among the 256 tokens of one device no expert is named more than 128 times, and in some device's tokens one expert is named exactly 128 times.
All inputs are finite; a program needn't handle non-finite values.
Results may differ from a plain program's by a relative error of at most 0.03.
Values may be sent and summed in bfloat16 or wider, within the bound.
No kernel may reach another device: no remote copies, remote signals or barrier semaphores. Data moves between devices by JAX's collectives and lax.ppermute only.
A program may use at most 256 MiB of HBM per device.

v0:
```python
import math

import jax
import jax.numpy as jnp
from jax import lax
from jax.sharding import PartitionSpec as P

HEADS = 12
BLOCK = 256


EPSILON = 1e-06
NEG_LARGE = -1e30


def times_transposed(former, latter):
    return lax.dot_general(
        former, latter, (((1,), (1,)), ((), ())), preferred_element_type=jnp.float32
    )


def transposed_times(former, latter):
    return lax.dot_general(
        former, latter, (((0,), (0,)), ((), ())), preferred_element_type=jnp.float32
    )


def rms_scale(values):
    return lax.rsqrt(jnp.mean(values * values, axis=1, keepdims=True) + EPSILON)


def norm_back(grad_normed, normed, scale_rows):
    return scale_rows * (
        grad_normed - normed * jnp.mean(grad_normed * normed, axis=1, keepdims=True)
    )


def silu_value(values):
    return values * jax.nn.sigmoid(values)


def silu_slope(values):
    logistic = jax.nn.sigmoid(values)
    return logistic * (1.0 + values * (1.0 - logistic))


def rotate(values, cosine_table, sine_table):
    halfway = values.shape[-1] // 2
    front_half = values[..., :halfway]
    back_half = values[..., halfway:]
    return jnp.concatenate(
        [
            front_half * cosine_table - back_half * sine_table,
            back_half * cosine_table + front_half * sine_table,
        ],
        axis=-1,
    )


def turn_tables(places, head_dim):
    halfway = head_dim // 2
    inverse = jnp.exp(
        jnp.arange(halfway).astype(jnp.float32) * (-2.0 * math.log(10000.0) / head_dim)
    )
    turned = places.astype(jnp.float32)[:, None] * inverse[None, :]
    return (jnp.cos(turned)[:, None, :], jnp.sin(turned)[:, None, :])


def allowed_pairs(query_segment, query_places, key_segment, key_places):
    same_doc = query_segment[:, None] == key_segment[None, :]
    earlier = key_places[None, :] // BLOCK <= query_places[:, None] // BLOCK
    return jnp.logical_and(same_doc, earlier)[None]


def shards(
    tokens,
    segment_ids,
    routes,
    norm1_gain,
    w_query,
    w_key,
    w_value,
    w_out,
    norm2_gain,
    w_router,
    shared_gate,
    shared_up,
    shared_down,
    expert_gate,
    expert_up,
    expert_down,
    out_grad,
):
    (
        first_norm_gain,
        query_matrix,
        key_matrix,
        value_matrix,
        output_matrix,
        second_norm_gain,
        router_matrix,
        shared_gate_full,
        shared_up_full,
        shared_down_full,
    ) = (
        lax.all_gather(norm1_gain, ("rep", "ep"), axis=0, tiled=True),
        lax.all_gather(w_query, ("rep", "ep"), axis=0, tiled=True),
        lax.all_gather(w_key, ("rep", "ep"), axis=0, tiled=True),
        lax.all_gather(w_value, ("rep", "ep"), axis=0, tiled=True),
        lax.all_gather(w_out, ("rep", "ep"), axis=0, tiled=True),
        lax.all_gather(norm2_gain, ("rep", "ep"), axis=0, tiled=True),
        lax.all_gather(w_router, ("rep", "ep"), axis=0, tiled=True),
        lax.all_gather(shared_gate, ("rep", "ep"), axis=0, tiled=True),
        lax.all_gather(shared_up, ("rep", "ep"), axis=0, tiled=True),
        lax.all_gather(shared_down, ("rep", "ep"), axis=0, tiled=True),
    )
    token_rows = tokens.shape[0]
    model_width = tokens.shape[1]
    head_count = HEADS
    head_dim = model_width // head_count
    score_scale = head_dim ** (-0.5)
    group_size = lax.axis_size("ep")
    whole_rows = token_rows * group_size
    step_rows = math.gcd(whole_rows, 512)
    top_count = routes.shape[1]
    experts = router_matrix.shape[1]
    local_experts = expert_gate.shape[0]
    capacity = 2 * token_rows * top_count // experts
    choice_count = token_rows * top_count
    places = lax.axis_index("ep") * token_rows + jnp.arange(token_rows, dtype=jnp.int32)
    cosine_table, sine_table = turn_tables(places, head_dim)
    own_segment = segment_ids.reshape(token_rows)
    layer_inputs = tokens.astype(jnp.float32)
    scale_first = rms_scale(layer_inputs)
    normed_first = layer_inputs * scale_first
    gain_first = first_norm_gain.astype(jnp.float32)
    hidden_first = (normed_first * gain_first).astype(jnp.bfloat16)
    query_raw = jnp.dot(hidden_first, query_matrix, preferred_element_type=jnp.float32).reshape(
        token_rows, head_count, head_dim
    )
    queries = rotate(query_raw, cosine_table, sine_table).astype(jnp.bfloat16)
    key_raw = jnp.dot(hidden_first, key_matrix, preferred_element_type=jnp.float32).reshape(
        token_rows, head_count, head_dim
    )
    keys_local = rotate(key_raw, cosine_table, sine_table).astype(jnp.bfloat16)
    values_local = (
        jnp.dot(hidden_first, value_matrix, preferred_element_type=jnp.float32)
        .astype(jnp.bfloat16)
        .reshape(token_rows, head_count, head_dim)
    )
    keys_flat = keys_local.reshape(token_rows, model_width)
    values_flat = values_local.reshape(token_rows, model_width)

    def key_update(carried, key_block, value_block, segment_block, block_start):
        running_max, running_total, running_acc = carried
        key_places = block_start + jnp.arange(key_block.shape[0], dtype=jnp.int32)
        allowed = allowed_pairs(own_segment, places, segment_block, key_places)
        scores = (
            jnp.einsum("qhd,khd->hqk", queries, key_block, preferred_element_type=jnp.float32)
            * score_scale
        )
        scores = jnp.where(allowed, scores, NEG_LARGE)
        new_max = jnp.maximum(running_max, jnp.max(scores, axis=2))
        factor = jnp.exp(running_max - new_max)
        weights = jnp.where(allowed, jnp.exp(scores - new_max[:, :, None]), 0.0)
        running_total = running_total * factor + jnp.sum(weights, axis=2)
        running_acc = running_acc * factor[:, :, None] + jnp.einsum(
            "hqk,khd->hqd",
            weights.astype(jnp.bfloat16),
            value_block,
            preferred_element_type=jnp.float32,
        )
        return (new_max, running_total, running_acc)

    start_state = (
        jnp.full((head_count, token_rows), NEG_LARGE, jnp.float32),
        jnp.zeros((head_count, token_rows), jnp.float32),
        jnp.zeros((head_count, token_rows, head_dim), jnp.float32),
    )
    carried = start_state
    key_piece = lax.all_gather(keys_flat, "ep", axis=0, tiled=True)
    value_piece = lax.all_gather(values_flat, "ep", axis=0, tiled=True)
    segment_piece = lax.all_gather(own_segment, "ep", axis=0, tiled=True)
    piece_rows = key_piece.shape[0]
    inner_rows = math.gcd(piece_rows, 512)

    def inner_step(inner_carried, block_index):
        offset = block_index * inner_rows
        key_block = lax.dynamic_slice_in_dim(key_piece, offset, inner_rows, 0).reshape(
            inner_rows, head_count, head_dim
        )
        value_block = lax.dynamic_slice_in_dim(value_piece, offset, inner_rows, 0).reshape(
            inner_rows, head_count, head_dim
        )
        segment_block = lax.dynamic_slice_in_dim(segment_piece, offset, inner_rows, 0)
        return (key_update(inner_carried, key_block, value_block, segment_block, offset), None)

    carried, unused = lax.scan(
        inner_step, carried, jnp.arange(piece_rows // inner_rows, dtype=jnp.int32)
    )
    final_max, final_total, final_acc = carried
    log_total = final_max + jnp.log(final_total)
    attended = final_acc / final_total[:, :, None]
    attended_low = (
        jnp.transpose(attended, (1, 0, 2)).reshape(token_rows, model_width).astype(jnp.bfloat16)
    )
    attn_result = jnp.dot(attended_low, output_matrix, preferred_element_type=jnp.float32)
    middle = layer_inputs + attn_result
    scale_second = rms_scale(middle)
    normed_second = middle * scale_second
    gain_second = second_norm_gain.astype(jnp.float32)
    hidden_second = (normed_second * gain_second).astype(jnp.bfloat16)
    logits = jnp.dot(hidden_second, router_matrix, preferred_element_type=jnp.float32)
    shifted = jnp.exp(logits - jnp.max(logits, axis=1, keepdims=True))
    router_probs = shifted / jnp.sum(shifted, axis=1, keepdims=True)
    route_table = (
        routes[:, :, None] == jnp.arange(experts, dtype=jnp.int32)[None, None, :]
    ).astype(jnp.float32)
    gate_values = jnp.sum(router_probs[:, None, :] * route_table, axis=2)
    shared_pre = jnp.dot(hidden_second, shared_gate_full, preferred_element_type=jnp.float32)
    shared_lin = jnp.dot(hidden_second, shared_up_full, preferred_element_type=jnp.float32)
    shared_hidden = (silu_value(shared_pre) * shared_lin).astype(jnp.bfloat16)
    shared_result = jnp.dot(shared_hidden, shared_down_full, preferred_element_type=jnp.float32)
    flat_routes = routes.reshape(choice_count)
    onehot = (flat_routes[:, None] == jnp.arange(experts, dtype=jnp.int32)[None, :]).astype(
        jnp.int32
    )
    own_rank = jnp.sum((jnp.cumsum(onehot, axis=0) - 1) * onehot, axis=1)
    slot_of_choice = flat_routes * capacity + own_rank
    slot_source = (
        jnp.full((experts * capacity,), choice_count, jnp.int32)
        .at[slot_of_choice]
        .set(jnp.arange(choice_count, dtype=jnp.int32))
    )
    slot_token_row = jnp.where(slot_source < choice_count, slot_source // top_count, token_rows)
    padded_rows = jnp.concatenate(
        [hidden_second, jnp.zeros((1, model_width), jnp.bfloat16)], axis=0
    )
    outgoing = padded_rows[slot_token_row].reshape(group_size, local_experts, capacity, model_width)
    received = lax.all_to_all(outgoing, "ep", split_axis=0, concat_axis=0, tiled=True)
    gate_pre = jnp.einsum(
        "sjcd,jdf->sjcf", received, expert_gate, preferred_element_type=jnp.float32
    )
    up_pre = jnp.einsum("sjcd,jdf->sjcf", received, expert_up, preferred_element_type=jnp.float32)
    expert_hidden = (silu_value(gate_pre) * up_pre).astype(jnp.bfloat16)
    expert_result = jnp.einsum(
        "sjcf,jfd->sjcd", expert_hidden, expert_down, preferred_element_type=jnp.float32
    ).astype(jnp.bfloat16)
    returned = lax.all_to_all(expert_result, "ep", split_axis=0, concat_axis=0, tiled=True).reshape(
        experts * capacity, model_width
    )
    picked = returned[slot_of_choice].reshape(token_rows, top_count, model_width)
    mixture = jnp.sum(gate_values[:, :, None] * picked.astype(jnp.float32), axis=1)
    layer_out = (middle + shared_result + mixture).astype(jnp.bfloat16)
    grad_output = out_grad.astype(jnp.float32)
    shared_hidden_grad = times_transposed(out_grad, shared_down_full)
    shared_pre_grad = (shared_hidden_grad * shared_lin * silu_slope(shared_pre)).astype(
        jnp.bfloat16
    )
    shared_lin_grad = (shared_hidden_grad * silu_value(shared_pre)).astype(jnp.bfloat16)
    choice_grad = (
        (gate_values[:, :, None] * grad_output[:, None, :])
        .astype(jnp.bfloat16)
        .reshape(choice_count, model_width)
    )
    padded_grads = jnp.concatenate([choice_grad, jnp.zeros((1, model_width), jnp.bfloat16)], axis=0)
    grads_outgoing = padded_grads[slot_source].reshape(
        group_size, local_experts, capacity, model_width
    )
    grads_received = lax.all_to_all(grads_outgoing, "ep", split_axis=0, concat_axis=0, tiled=True)
    expert_hidden_grad = jnp.einsum(
        "sjcd,jfd->sjcf", grads_received, expert_down, preferred_element_type=jnp.float32
    )
    gate_pre_grad = (expert_hidden_grad * up_pre * silu_slope(gate_pre)).astype(jnp.bfloat16)
    up_pre_grad = (expert_hidden_grad * silu_value(gate_pre)).astype(jnp.bfloat16)
    row_grads = (
        jnp.einsum("sjcf,jdf->sjcd", gate_pre_grad, expert_gate, preferred_element_type=jnp.float32)
        + jnp.einsum("sjcf,jdf->sjcd", up_pre_grad, expert_up, preferred_element_type=jnp.float32)
    ).astype(jnp.bfloat16)
    expert_gate_term = jnp.einsum(
        "sjcd,sjcf->jdf", received, gate_pre_grad, preferred_element_type=jnp.float32
    )
    expert_up_term = jnp.einsum(
        "sjcd,sjcf->jdf", received, up_pre_grad, preferred_element_type=jnp.float32
    )
    expert_down_term = jnp.einsum(
        "sjcf,sjcd->jfd", expert_hidden, grads_received, preferred_element_type=jnp.float32
    )
    rows_back = lax.all_to_all(row_grads, "ep", split_axis=0, concat_axis=0, tiled=True).reshape(
        experts * capacity, model_width
    )
    gate_grad = jnp.sum(grad_output[:, None, :] * picked.astype(jnp.float32), axis=2)
    prob_grad = jnp.sum(gate_grad[:, :, None] * route_table, axis=1)
    logit_grad = (
        router_probs * (prob_grad - jnp.sum(router_probs * prob_grad, axis=1, keepdims=True))
    ).astype(jnp.bfloat16)
    second_grad = (
        times_transposed(shared_pre_grad, shared_gate_full)
        + times_transposed(shared_lin_grad, shared_up_full)
        + times_transposed(logit_grad, router_matrix)
    )
    second_grad = second_grad + jnp.sum(
        rows_back[slot_of_choice].reshape(token_rows, top_count, model_width).astype(jnp.float32),
        axis=1,
    )
    router_term = transposed_times(hidden_second, logit_grad)
    shared_gate_term = transposed_times(hidden_second, shared_pre_grad)
    shared_up_term = transposed_times(hidden_second, shared_lin_grad)
    shared_down_term = transposed_times(shared_hidden, out_grad)
    gain_second_term = jnp.sum(second_grad * normed_second, axis=0)
    middle_grad = grad_output + norm_back(second_grad * gain_second, normed_second, scale_second)
    attn_grad = middle_grad.astype(jnp.bfloat16)
    output_term = transposed_times(attended_low, attn_grad)
    attended_grad = times_transposed(attn_grad, output_matrix).astype(jnp.bfloat16)
    grad_heads = attended_grad.reshape(token_rows, head_count, head_dim)
    row_delta = jnp.einsum("qhd,hqd->hq", grad_heads.astype(jnp.float32), attended)
    key_whole, value_whole, segment_whole = (
        lax.all_gather(keys_flat, "ep", axis=0, tiled=True),
        lax.all_gather(values_flat, "ep", axis=0, tiled=True),
        lax.all_gather(own_segment, "ep", axis=0, tiled=True),
    )

    def key_back(query_acc, block_index):
        offset = block_index * step_rows
        key_block = lax.dynamic_slice_in_dim(key_whole, offset, step_rows, 0).reshape(
            step_rows, head_count, head_dim
        )
        value_block = lax.dynamic_slice_in_dim(value_whole, offset, step_rows, 0).reshape(
            step_rows, head_count, head_dim
        )
        segment_block = lax.dynamic_slice_in_dim(segment_whole, offset, step_rows, 0)
        key_places = offset + jnp.arange(step_rows, dtype=jnp.int32)
        allowed = allowed_pairs(own_segment, places, segment_block, key_places)
        scores = (
            jnp.einsum("qhd,khd->hqk", queries, key_block, preferred_element_type=jnp.float32)
            * score_scale
        )
        probs_exact = jnp.where(allowed, jnp.exp(scores - log_total[:, :, None]), 0.0)
        prob_grads = jnp.einsum(
            "qhd,khd->hqk", grad_heads, value_block, preferred_element_type=jnp.float32
        )
        score_grads = (probs_exact * (prob_grads - row_delta[:, :, None])).astype(jnp.bfloat16)
        query_acc = query_acc + jnp.einsum(
            "hqk,khd->qhd", score_grads, key_block, preferred_element_type=jnp.float32
        )
        key_part = jnp.einsum(
            "hqk,qhd->khd", score_grads, queries, preferred_element_type=jnp.float32
        ).reshape(step_rows, model_width)
        value_part = jnp.einsum(
            "hqk,qhd->khd",
            probs_exact.astype(jnp.bfloat16),
            grad_heads,
            preferred_element_type=jnp.float32,
        ).reshape(step_rows, model_width)
        return (query_acc, jnp.concatenate([key_part, value_part], axis=1))

    query_acc, key_terms = lax.scan(
        key_back,
        jnp.zeros((token_rows, head_count, head_dim), jnp.float32),
        jnp.arange(whole_rows // step_rows, dtype=jnp.int32),
    )
    key_value_sum = lax.psum_scatter(
        key_terms.reshape(whole_rows, 2 * model_width).astype(jnp.bfloat16),
        "ep",
        scatter_dimension=0,
        tiled=True,
    ).astype(jnp.float32)
    query_sum = query_acc.reshape(token_rows, model_width)
    key_sum = key_value_sum[:, :model_width]
    value_sum = key_value_sum[:, model_width:]
    query_grad = (
        rotate(
            (query_sum * score_scale).reshape(token_rows, head_count, head_dim),
            cosine_table,
            -sine_table,
        )
        .astype(jnp.bfloat16)
        .reshape(token_rows, model_width)
    )
    key_grad = (
        rotate(
            (key_sum * score_scale).reshape(token_rows, head_count, head_dim),
            cosine_table,
            -sine_table,
        )
        .astype(jnp.bfloat16)
        .reshape(token_rows, model_width)
    )
    value_grad = value_sum.astype(jnp.bfloat16)
    first_grad = (
        times_transposed(query_grad, query_matrix)
        + times_transposed(key_grad, key_matrix)
        + times_transposed(value_grad, value_matrix)
    )
    query_term = transposed_times(hidden_first, query_grad)
    key_term = transposed_times(hidden_first, key_grad)
    value_term = transposed_times(hidden_first, value_grad)
    gain_first_term = jnp.sum(first_grad * normed_first, axis=0)
    tokens_grad = middle_grad + norm_back(first_grad * gain_first, normed_first, scale_first)
    dense_grads = (
        lax.psum_scatter(gain_first_term, ("rep", "ep"), scatter_dimension=0, tiled=True),
        lax.psum_scatter(query_term, ("rep", "ep"), scatter_dimension=0, tiled=True),
        lax.psum_scatter(key_term, ("rep", "ep"), scatter_dimension=0, tiled=True),
        lax.psum_scatter(value_term, ("rep", "ep"), scatter_dimension=0, tiled=True),
        lax.psum_scatter(output_term, ("rep", "ep"), scatter_dimension=0, tiled=True),
        lax.psum_scatter(gain_second_term, ("rep", "ep"), scatter_dimension=0, tiled=True),
        lax.psum_scatter(router_term, ("rep", "ep"), scatter_dimension=0, tiled=True),
        lax.psum_scatter(shared_gate_term, ("rep", "ep"), scatter_dimension=0, tiled=True),
        lax.psum_scatter(shared_up_term, ("rep", "ep"), scatter_dimension=0, tiled=True),
        lax.psum_scatter(shared_down_term, ("rep", "ep"), scatter_dimension=0, tiled=True),
    )
    expert_grads = (
        lax.psum_scatter(
            expert_gate_term.astype(jnp.bfloat16), "rep", scatter_dimension=2, tiled=True
        ).astype(jnp.float32),
        lax.psum_scatter(
            expert_up_term.astype(jnp.bfloat16), "rep", scatter_dimension=2, tiled=True
        ).astype(jnp.float32),
        lax.psum_scatter(
            expert_down_term.astype(jnp.bfloat16), "rep", scatter_dimension=2, tiled=True
        ).astype(jnp.float32),
    )
    return (
        layer_out,
        tokens_grad,
        dense_grads[0],
        dense_grads[1],
        dense_grads[2],
        dense_grads[3],
        dense_grads[4],
        dense_grads[5],
        dense_grads[6],
        dense_grads[7],
        dense_grads[8],
        dense_grads[9],
        expert_grads[0],
        expert_grads[1],
        expert_grads[2],
    )


def solution(mesh):
    return jax.shard_map(
        shards,
        mesh=mesh,
        in_specs=(
            P(("rep", "ep"), None),
            P("rep", "ep"),
            P(("rep", "ep"), None),
            P(("rep", "ep")),
            P(("rep", "ep"), None),
            P(("rep", "ep"), None),
            P(("rep", "ep"), None),
            P(("rep", "ep"), None),
            P(("rep", "ep")),
            P(("rep", "ep"), None),
            P(("rep", "ep"), None),
            P(("rep", "ep"), None),
            P(("rep", "ep"), None),
            P("ep", None, None),
            P("ep", None, None),
            P("ep", None, None),
            P(("rep", "ep"), None),
        ),
        out_specs=(
            P(("rep", "ep"), None),
            P(("rep", "ep"), None),
            P(("rep", "ep")),
            P(("rep", "ep"), None),
            P(("rep", "ep"), None),
            P(("rep", "ep"), None),
            P(("rep", "ep"), None),
            P(("rep", "ep")),
            P(("rep", "ep"), None),
            P(("rep", "ep"), None),
            P(("rep", "ep"), None),
            P(("rep", "ep"), None),
            P("ep", None, "rep"),
            P("ep", None, "rep"),
            P("ep", None, "rep"),
        ),
        check_vma=False,
    )
```

profile of v0, /device:TPU:0, one launch (start us, length us, event | category | flops | bytes accessed | tf_op | source)
XLA Modules:
  0.0 1671.8 jit_solution(3728425969518155587)
XLA Ops:
  11.2 42.0 %all-reduce.8 = (bf16[768]{0:T(1024)(128)(2,1)S(1)}, bf16[768]{0:T(1024)(128)(2,1)}) all-reduce(bf16[768]{0:T(1024)(128)(2,1)S(1)} %dynamic-update-slice, bf16[768]{0:T(1024)(128)(2,1)S(1)} %dynamic-update-slice.1), channel_id=1, replica_groups=mesh['rep'=4,'ep'=8] {'rep','ep'}, use_global_device_ids=true, to_apply=%add.2 | all-reduce | flops 1536 | bytes 6144
  54.4 13.5 all-gather.18.cloned.1.call-done
  71.5 52.5 %all-gather.16.cloned.1.call-done = bf16[768,768]{1,0:T(8,128)(2,1)} async-done(((bf16[24,768]{1,0:T(8,128)(2,1)}), bf16[768,768]{1,0:T(8,128)(2,1)}) %all-gather.16.cloned.1.call-update) | async-done | bytes 1179664 | tf_op jit(solution)/shard_map/all_gather | solution.py:107
  126.7 53.3 %all-gather.12.cloned.1.call-done = bf16[768,768]{1,0:T(8,128)(2,1)} async-done(((bf16[24,768]{1,0:T(8,128)(2,1)}), bf16[768,768]{1,0:T(8,128)(2,1)}) %all-gather.12.cloned.1.call-update) | async-done | bytes 1179664 | tf_op jit(solution)/shard_map/all_gather | solution.py:108
  197.7 11.9 all-gather
  210.2 38.1 %all-gather.1 = bf16[32,24,8]{1,2,0:T(8,128)(2,1)S(1)} all-gather(bf16[1,24,8]{1,2,0:T(8,128)(2,1)S(1)} %bitcast.382), channel_id=1, replica_groups=mesh['rep'=4,'ep'=8] {'rep','ep'}, dimensions={0}, use_global_device_ids=true | all-gather | bytes 12672 | tf_op jit(solution)/shard_map/all_gather | solution.py:112
  255.3 4.9 copy.126
  260.7 83.6 %while.38 = (s32[]{:T(128)}, f32[12,256]{1,0:T(8,128)S(1)}, f32[12,256]{1,0:T(8,128)}, f32[12,256,64]{1,2,0:T(8,128)}, s32[1,256]{1,0:T(1,128)}, /*index=5*/s32[...) while((s32[]{:T(128)}, f32[12,256]{1,0:T(8,128)S(1)}, ...), condition=%wide.region_4.5_spmd.clone.clone.clone, body=%wide.region_1.4_spmd.clone.clone.clone.sunk | while | flops 424111616 | bytes 52608892 | solution.py:198
  267.8 4.4 fusion.238
  273.0 4.4 fusion.239
  288.6 4.4 fusion.238
  309.5 4.4 fusion.238
  330.5 4.4 fusion.238
  357.8 7.0 gather_fusion.2
  364.8 4.4 all-to-all-start.2
  370.3 5.2 gather_fusion
  375.5 34.3 %all-to-all-done.2 = bf16[8,1,128,768]{3,2,1,0:T(8,128)(2,1)} async-done(((bf16[8,1,128,768]{3,2,1,0:T(8,128)(2,1)}), bf16[8,1,128,768]{3,2,1,0:T(8,128)(2,1)}, u32[]{:S(2)}, u32[]{:S(2)}) %all-to-all-start.2) | async-done | bytes 1572896 | tf_op jit(solution)/shard_map/all_to_all | solution.py:270
  414.8 9.1 fusion.61
  424.0 39.7 %all-to-all-done = bf16[8,1,128,768]{3,2,1,0:T(8,128)(2,1)} async-done(((bf16[8,1,128,768]{3,2,1,0:T(8,128)(2,1)}), bf16[8,1,128,768]{3,2,1,0:T(8,128)(2,1)}, u32[]{:S(2)}, u32[]{:S(2)}) %all-to-all-start) | async-done | bytes 1572896 | tf_op jit(solution)/shard_map/all_to_all | solution.py:240
  463.7 5.8 fusion.67
  469.5 12.8 fusion.54
  482.3 6.8 fusion.89
  489.1 4.6 all-to-all-start.1
  493.7 5.5 fusion.57
  499.2 4.6 fusion.92
  503.8 37.8 %all-to-all-done.1 = bf16[8,1,128,768]{3,2,1,0:T(8,128)(2,1)} async-done(((bf16[8,1,128,768]{3,2,1,0:T(8,128)(2,1)}), bf16[8,1,128,768]{3,2,1,0:T(8,128)(2,1)}, u32[]{:S(2)}, u32[]{:S(2)}) %all-to-all-start.1) | async-done | bytes 1572896 | tf_op jit(solution)/shard_map/all_to_all | solution.py:249
  554.4 5.8 multiply_convert_fusion
  564.9 5.2 gather_fusion.1
  573.0 9.9 all-to-all-done.3
  588.6 5.0 multiply_reduce_fusion
  601.3 77.5 %while.39 = (s32[]{:T(128)}, f32[256,12,64]{0,2,1:T(8,128)}, bf16[4,512,1536]{2,1,0:T(8,128)(2,1)}, s32[4]{0:T(128)S(1)}, bf16[2048,768]{0,1:T(8,128)(2,1)}, /*i...) while((s32[]{:T(128)}, f32[256,12,64]{0,2,1:T(8,128)}, ...), condition=%wide.region_20.21_spmd.clone.clone.clone, body=%wide.region_19.20_spmd.clone.clone.clone.sunk | while | flops 1026306560 | bytes 81072312 | solution.py:357
  678.9 6.2 fusion.76
  685.1 11.6 copy.164
  696.6 6.5 copy.184
  703.2 7.8 fusion.72
  711.1 7.8 fusion.75
  737.2 9.6 reduce-scatter.15.cloned.1.call-done
  760.6 31.6 %reduce-scatter.35.cloned.1.call-done = bf16[192,2048]{1,0:T(8,128)(2,1)} async-done(((bf16[768,2048]{1,0:T(8,128)(2,1)}), bf16[192,2048]{1,0:T(8,128)(2,1)}) %reduce-scatter.35.cloned.1.call-update) | async-done | bytes 786448
  797.7 41.3 %reduce-scatter.31.cloned.1.call-done = bf16[1,768,512]{2,1,0:T(8,128)(2,1)} async-done(((bf16[1,768,2048]{2,1,0:T(8,128)(2,1)}), bf16[1,768,512]{2,1,0:T(8,128)(2,1)}) %reduce-scatter.31.cloned.1.call-update) | async-done | bytes 786448 | tf_op jit(solution)/shard_map/reduce_scatter | solution.py:413
  841.5 44.4 %reduce-scatter.33.cloned.1.call-done = bf16[1,768,512]{2,1,0:T(8,128)(2,1)} async-done(((bf16[1,768,2048]{2,1,0:T(8,128)(2,1)}), bf16[1,768,512]{2,1,0:T(8,128)(2,1)}) %reduce-scatter.33.cloned.1.call-update) | async-done | bytes 786448 | tf_op jit(solution)/shard_map/reduce_scatter | solution.py:416
  893.1 40.3 %all-reduce.7 = (f32[768]{0:T(1024)}, f32[768]{0:T(1024)}, f32[768,8]{0,1:T(8,128)}) all-reduce(f32[768]{0:T(1024)S(1)} %get-tuple-element.848, f32[768]{0:T(1024)S(1)} %copy-done.66, f32[768,8]{0,1:T(8,128)} %fusion.150), channel_id=4, replica_groups=mesh['rep'=4,'ep'=8] {'rep','ep'}, use_global_device_ids=true, to_apply=%region_24.25.clone | all-reduce | flops 7680 | bytes 61440
  940.4 66.5 %reduce-scatter.25.cloned.1.call-done = f32[24,2048]{1,0:T(8,128)} async-done(((f32[768,2048]{1,0:T(8,128)}), f32[24,2048]{1,0:T(8,128)}) %reduce-scatter.25.cloned.1.call-update) | async-done | bytes 196624 | tf_op jit(solution)/shard_map/reduce_scatter | solution.py:408
  1006.9 120.0 %reduce-scatter.27.cloned.1.call-done = f32[24,2048]{1,0:T(8,128)} async-done(((f32[768,2048]{1,0:T(8,128)}), f32[24,2048]{1,0:T(8,128)}) %reduce-scatter.27.cloned.1.call-update) | async-done | bytes 196624 | tf_op jit(solution)/shard_map/reduce_scatter | solution.py:409
  1126.9 120.1 %reduce-scatter.29.cloned.1.call-done = f32[64,768]{1,0:T(8,128)} async-done(((f32[2048,768]{1,0:T(8,128)}), f32[64,768]{1,0:T(8,128)}) %reduce-scatter.29.cloned.1.call-update) | async-done | bytes 196624 | tf_op jit(solution)/shard_map/reduce_scatter | solution.py:410
  1247.0 104.3 %reduce-scatter.23.cloned.1.call-done = f32[24,768]{1,0:T(8,128)} async-done(((f32[768,768]{1,0:T(8,128)}), f32[24,768]{1,0:T(8,128)}) %reduce-scatter.23.cloned.1.call-update) | async-done | bytes 73744 | tf_op jit(solution)/shard_map/reduce_scatter | solution.py:405
  1351.3 104.4 %reduce-scatter.17.cloned.1.call-done = f32[24,768]{1,0:T(8,128)} async-done(((f32[768,768]{1,0:T(8,128)}), f32[24,768]{1,0:T(8,128)}) %reduce-scatter.17.cloned.1.call-update) | async-done | bytes 73744 | tf_op jit(solution)/shard_map/reduce_scatter | solution.py:402
  1455.6 104.5 %reduce-scatter.19.cloned.1.call-done = f32[24,768]{1,0:T(8,128)} async-done(((f32[768,768]{1,0:T(8,128)}), f32[24,768]{1,0:T(8,128)}) %reduce-scatter.19.cloned.1.call-update) | async-done | bytes 73744 | tf_op jit(solution)/shard_map/reduce_scatter | solution.py:403
  1560.1 104.4 %reduce-scatter.21.cloned.1.call-done = f32[24,768]{1,0:T(8,128)} async-done(((f32[768,768]{1,0:T(8,128)}), f32[24,768]{1,0:T(8,128)}) %reduce-scatter.21.cloned.1.call-update) | async-done | bytes 73744 | tf_op jit(solution)/shard_map/reduce_scatter | solution.py:404
  (536 shorter events, 276.7 us)
Async XLA Ops:
  7.2 462.3 %copy-start = (bf16[1,768,2048]{2,1,0:T(8,128)(2,1)S(1)}, bf16[1,768,2048]{2,1,0:T(8,128)(2,1)}, u32[]{:S(2)}) copy-start(bf16[1,768,2048]{2,1,0:T(8,128)(2,1)} %param.34) | copy-start | bytes 9437188
  7.2 116.8 %copy-start.7 = (bf16[256,768]{1,0:T(8,128)(2,1)S(1)}, bf16[256,768]{1,0:T(8,128)(2,1)}, u32[]{:S(2)}) copy-start(bf16[256,768]{1,0:T(8,128)(2,1)} %param.21) | copy-start | bytes 1179652
  7.2 60.7 %all-gather.18.cloned.1.call-start = ((), (), s32[]{:S(2)}) async-start(), calls=%async_computation.18 | async-start | bytes 1216512 | tf_op jit(solution)/shard_map/all_gather | solution.py:109
  7.9 116.0 %all-gather.16.cloned.1.call-start = ((), (), s32[]{:S(2)}) async-start(), calls=%async_computation.17 | async-start | bytes 1216512 | tf_op jit(solution)/shard_map/all_gather | solution.py:107
  8.7 171.3 %all-gather.12.cloned.1.call-start = ((), (), s32[]{:S(2)}) async-start(), calls=%async_computation.15 | async-start | bytes 1216512 | tf_op jit(solution)/shard_map/all_gather | solution.py:108
  9.4 245.9 %all-gather.20.cloned.1.call-start = ((), (), s32[]{:S(2)}) async-start(), calls=%async_computation.19 | async-start | bytes 3538944 | tf_op jit(solution)/shard_map/all_gather | solution.py:182
  53.2 128.7 %copy-start.49 = (f32[768]{0:T(1024)}, f32[768]{0:T(1024)S(1)}, u32[]{:S(2)}) copy-start(f32[768]{0:T(1024)S(1)} %convert_element_type.199) | copy-start | bytes 9220
  54.4 127.6 %copy-start.56 = (f32[256]{0:T(256)}, f32[256]{0:T(256)S(1)}, u32[]{:S(2)}) copy-start(f32[256]{0:T(256)S(1)} %add_rsqrt_fusion.1) | copy-start | bytes 3076
  70.6 189.6 %all-gather.14.cloned.1.call-start = ((), (), s32[]{:S(2)}) async-start(), calls=%async_computation.16 | async-start | bytes 3538944 | tf_op jit(solution)/shard_map/all_gather | solution.py:181
  184.9 161.5 %all-gather.22.cloned.1.call-start = ((), (), s32[]{:S(2)}) async-start(), calls=%async_computation.20 | async-start | bytes 1216512 | tf_op jit(solution)/shard_map/all_gather | solution.py:110
  185.5 360.4 %all-gather.24.cloned.1.call-start = ((), (), s32[]{:S(2)}) async-start(), calls=%async_computation.21 | async-start | bytes 3244032 | tf_op jit(solution)/shard_map/all_gather | solution.py:113
  186.2 363.9 %all-gather.26.cloned.1.call-start = ((), (), s32[]{:S(2)}) async-start(), calls=%async_computation.22 | async-start | bytes 3244032 | tf_op jit(solution)/shard_map/all_gather | solution.py:114
  194.5 15.1 copy-start.80
  194.5 15.7 copy-start.79
  194.5 54.6 %copy-start.75 = (s32[256,2]{0,1:T(2,128)S(1)}, s32[256,2]{0,1:T(2,128)}, u32[]{:S(2)}) copy-start(s32[256,2]{0,1:T(2,128)} %broadcast_multiply_fusion.1) | copy-start | bytes 6148
  194.5 54.9 %copy-start.74 = (s32[4,128]{1,0:T(4,128)S(1)}, s32[4,128]{1,0:T(4,128)}, u32[]{:S(2)}) copy-start(s32[4,128]{1,0:T(4,128)} %eq.91) | copy-start | bytes 6148
  194.5 56.3 %copy-start.76 = (s32[512]{0:T(512)S(1)}, s32[512]{0:T(512)}, u32[]{:S(2)}) copy-start(s32[512]{0:T(512)} %eq.87) | copy-start | bytes 6148
  344.3 12.5 copy-start.5
  344.3 12.5 copy-start.34
  364.8 45.0 %all-to-all-start.2 = ((bf16[8,1,128,768]{3,2,1,0:T(8,128)(2,1)}), bf16[8,1,128,768]{3,2,1,0:T(8,128)(2,1)}, u32[]{:S(2)}, u32[]{:S(2)}) async-start(bf16[8,1,128,768]{3,2,1,0:T(8,128)(2,1)} %bitcast.364), calls=%async_computation.2 | async-start | bytes 3145728 | tf_op jit(solution)/shard_map/all_to_all | solution.py:270
  409.8 53.9 %all-to-all-start = ((bf16[8,1,128,768]{3,2,1,0:T(8,128)(2,1)}), bf16[8,1,128,768]{3,2,1,0:T(8,128)(2,1)}, u32[]{:S(2)}, u32[]{:S(2)}) async-start(bf16[8,1,128,768]{3,2,1,0:T(8,128)(2,1)} %bitcast.363), calls=%async_computation | async-start | bytes 3145728 | tf_op jit(solution)/shard_map/all_to_all | solution.py:240
  414.1 140.3 %all-gather.28.cloned.1.call-start = ((), (), s32[]{:S(2)}) async-start(), calls=%async_computation.23 | async-start | bytes 3244032 | tf_op jit(solution)/shard_map/all_gather | solution.py:115
  469.5 12.8 copy-start.81
  489.1 52.5 %all-to-all-start.1 = ((bf16[8,1,128,768]{3,2,1,0:T(8,128)(2,1)}), bf16[8,1,128,768]{3,2,1,0:T(8,128)(2,1)}, u32[]{:S(2)}, u32[]{:S(2)}) async-start(bf16[8,1,128,768]{3,2,1,0:T(8,128)(2,1)} %fusion.89), calls=%async_computation.1 | async-start | bytes 3145728 | tf_op jit(solution)/shard_map/all_to_all | solution.py:249
  503.8 41.4 %copy-start.21 = (bf16[256,768]{1,0:T(8,128)(2,1)S(1)}, bf16[256,768]{1,0:T(8,128)(2,1)}, u32[]{:S(2)}) copy-start(bf16[256,768]{1,0:T(8,128)(2,1)} %param.37) | copy-start | bytes 1179652
  503.8 41.5 %copy-start.78 = (s32[512,1]{0,1:T(1,128)S(1)}, s32[512,1]{0,1:T(1,128)}, u32[]{:S(2)}) copy-start(s32[512,1]{0,1:T(1,128)} %copy-done.77) | copy-start | bytes 6148
  503.8 41.5 %copy-start.35 = (f32[12,256]{1,0:T(8,128)S(1)}, f32[12,256]{1,0:T(8,128)}, u32[]{:S(2)}) copy-start(f32[12,256]{1,0:T(8,128)} %copy-done.34) | copy-start | bytes 36868
  503.8 41.5 %copy-start.43 = (f32[12,256]{1,0:T(8,128)S(1)}, f32[12,256]{1,0:T(8,128)}, u32[]{:S(2)}) copy-start(f32[12,256]{1,0:T(8,128)} %get-tuple-element.419) | copy-start | bytes 36868
  503.8 42.2 %copy-start.10 = (bf16[256,768]{1,0:T(8,128)(2,1)S(1)}, bf16[256,768]{1,0:T(8,128)(2,1)}, u32[]{:S(2)}) copy-start(bf16[256,768]{1,0:T(8,128)(2,1)} %copy-done.9) | copy-start | bytes 1179652
  541.5 41.3 %all-to-all-start.3 = ((bf16[8,1,128,768]{3,2,1,0:T(8,128)(2,1)}), bf16[8,1,128,768]{3,2,1,0:T(8,128)(2,1)S(1)}, u32[]{:S(2)}, u32[]{:S(2)}) async-start(bf16[8,1,128,768]{3,2,1,0:T(8,128)(2,1)} %fusion.92), calls=%async_computation.3 | async-start | bytes 3145728 | tf_op jit(solution)/shard_map/all_to_all | solution.py:289
  545.1 201.7 %reduce-scatter.15.cloned.1.call-start = ((), (), s32[]{:S(2)}) async-start(), calls=%async_computation.24 | async-start | bytes 7077888 | tf_op jit(solution)/shard_map/reduce_scatter | solution.py:362
  678.8 113.4 %reduce-scatter.35.cloned.1.call-start = ((), (), s32[]{:S(2)}) async-start(), calls=%async_computation.34 | async-start | bytes 3932160
  703.1 135.9 %reduce-scatter.31.cloned.1.call-start = ((), (), s32[]{:S(2)}) async-start(), calls=%async_computation.32 | async-start | bytes 3932160 | tf_op jit(solution)/shard_map/reduce_scatter | solution.py:413
  711.0 174.9 %reduce-scatter.33.cloned.1.call-start = ((), (), s32[]{:S(2)}) async-start(), calls=%async_computation.33 | async-start | bytes 3932160 | tf_op jit(solution)/shard_map/reduce_scatter | solution.py:416
  718.9 288.0 %reduce-scatter.25.cloned.1.call-start = ((), (), s32[]{:S(2)}) async-start(), calls=%async_computation.29 | async-start | bytes 6488064 | tf_op jit(solution)/shard_map/reduce_scatter | solution.py:408
  724.0 402.9 %reduce-scatter.27.cloned.1.call-start = ((), (), s32[]{:S(2)}) async-start(), calls=%async_computation.30 | async-start | bytes 6488064 | tf_op jit(solution)/shard_map/reduce_scatter | solution.py:409
  728.9 518.1 %reduce-scatter.29.cloned.1.call-start = ((), (), s32[]{:S(2)}) async-start(), calls=%async_computation.31 | async-start | bytes 6488064 | tf_op jit(solution)/shard_map/reduce_scatter | solution.py:410
  733.9 617.4 %reduce-scatter.23.cloned.1.call-start = ((), (), s32[]{:S(2)}) async-start(), calls=%async_computation.28 | async-start | bytes 2433024 | tf_op jit(solution)/shard_map/reduce_scatter | solution.py:405
  737.0 11.1 copy-start.48
  737.0 11.1 copy-start.53
  737.1 718.6 %reduce-scatter.17.cloned.1.call-start = ((), (), s32[]{:S(2)}) async-start(), calls=%async_computation.25 | async-start | bytes 2433024 | tf_op jit(solution)/shard_map/reduce_scatter | solution.py:402
  737.2 11.3 copy-start.8
  737.2 11.3 copy-start.50
  737.2 11.3 copy-start.57
  750.6 809.5 %reduce-scatter.19.cloned.1.call-start = ((), (), s32[]{:S(2)}) async-start(), calls=%async_computation.26 | async-start | bytes 2433024 | tf_op jit(solution)/shard_map/reduce_scatter | solution.py:403
  752.7 911.8 %reduce-scatter.21.cloned.1.call-start = ((), (), s32[]{:S(2)}) async-start(), calls=%async_computation.27 | async-start | bytes 2433024 | tf_op jit(solution)/shard_map/reduce_scatter | solution.py:404
  796.3 92.1 %copy-start.24 = (bf16[768,768]{1,0:T(8,128)(2,1)S(1)}, bf16[768,768]{1,0:T(8,128)(2,1)}, u32[]{:S(2)}) copy-start(bf16[768,768]{1,0:T(8,128)(2,1)} %all-gather.16.cloned.1.call-done) | copy-start | bytes 3538948
  889.0 775.5 %copy-start.1 = (bf16[1,768,2048]{2,1,0:T(8,128)(2,1)S(1)}, bf16[1,768,2048]{2,1,0:T(8,128)(2,1)}, u32[]{:S(2)}) copy-start(bf16[1,768,2048]{2,1,0:T(8,128)(2,1)} %param.34) | copy-start | bytes 9437188
  (110 other events, 411.1 us)
Sparse Core Ops, SparseCore 0:
  11.0 56.8 all-gather.17
  70.9 52.9 all-gather.15
  127.0 52.9 all-gather.11
  182.1 37.2 all-gather.19
  221.4 38.3 all-gather.13
  262.6 52.4 all-gather.21
  318.1 58.9 all-gather.23
  380.2 81.1 all-gather.25
  464.4 73.4 all-gather.27
  678.9 67.8 reduce-scatter.14
  749.8 42.3 reduce-scatter.34
  795.1 43.8 reduce-scatter.30
  842.0 43.8 reduce-scatter.32
  892.0 114.8 reduce-scatter.24
  1012.9 113.8 reduce-scatter.26
  1132.9 113.9 reduce-scatter.28
  1252.7 98.5 reduce-scatter.22
  1357.0 98.6 reduce-scatter.16
  1461.5 98.6 reduce-scatter.18
  1565.8 98.6 reduce-scatter.20
where the time goes:
time: 1680 us; the launch traced here: 1670 us
  waiting for transfers between devices  1100 us (65%)
  matrix products  209 us (12%)
  blocking collectives  132 us (8%)
  local copies, waits for them, and re-layouts  126 us (8%)
  other arithmetic  67.8 us (4%)
  starting transfers between devices  18.2 us (1%)
    reduce_scatter x1, waiting for transfers between devices, shards(): lax.psum_scatter(shared_down_term, ('rep', 'ep'), scatter_dimension=0, ti...  120 us
    reduce_scatter x1, waiting for transfers between devices, shards(): lax.psum_scatter(shared_up_term, ('rep', 'ep'), scatter_dimension=0, tile...  120 us
    reduce_scatter x1, waiting for transfers between devices, shards(): lax.psum_scatter(key_term, ('rep', 'ep'), scatter_dimension=0, tiled=True)  105 us
    reduce_scatter x1, waiting for transfers between devices, shards(): lax.psum_scatter(query_term, ('rep', 'ep'), scatter_dimension=0, tiled=True)  104 us
    reduce_scatter x1, waiting for transfers between devices, shards(): lax.psum_scatter(value_term, ('rep', 'ep'), scatter_dimension=0, tiled=True)  104 us
    reduce_scatter x1, waiting for transfers between devices, shards(): lax.psum_scatter(output_term, ('rep', 'ep'), scatter_dimension=0, tiled=T...  104 us
    unnamed x2, blocking collectives  82.3 us
    reduce_scatter x1, waiting for transfers between devices, shards(): lax.psum_scatter(shared_gate_term, ('rep', 'ep'), scatter_dimension=0, ti...  66.5 us
  transfers between devices with their start and end apart: 24, of which 18 were waited for; matrix products, arithmetic and copies ran while one was open for 18% of the time, Pallas kernels for 0%

commit v1 on v0

v1 whole, which is shorter than its diff:
```python
import math

import jax
import jax.numpy as jnp
from jax import lax
from jax.experimental import pallas as pl
from jax.experimental.pallas import tpu as pltpu
from jax.sharding import PartitionSpec as P

HEADS = 12
HEAD_DIM = 64
SLAB = 2 * HEAD_DIM
EPSILON = 1e-06
NEG_LARGE = -1e30
BF = jnp.bfloat16
F32 = jnp.float32
ALL = ("rep", "ep")


def dot(a, b):
    return lax.dot_general(a, b, (((1,), (0,)), ((), ())), preferred_element_type=F32)


def dot_nt(a, b):
    return lax.dot_general(a, b, (((1,), (1,)), ((), ())), preferred_element_type=F32)


def dot_tn(a, b):
    return lax.dot_general(a, b, (((0,), (0,)), ((), ())), preferred_element_type=F32)


def rms_scale(values):
    return lax.rsqrt(jnp.mean(values * values, axis=1, keepdims=True) + EPSILON)


def swap_halves(values):
    width = values.shape[1]
    half = HEAD_DIM // 2
    lane = lax.broadcasted_iota(jnp.int32, values.shape, 1)
    return jnp.where(
        lane % HEAD_DIM < half,
        pltpu.roll(values, width - half, 1),
        pltpu.roll(values, half, 1),
    )


def head_mask(rows, head):
    lane = lax.broadcasted_iota(jnp.int32, (rows, SLAB), 1)
    return jnp.where(lane // HEAD_DIM == head, 1.0, 0.0).astype(BF)


def project_kernel(x_ref, w_ref, g_ref, cos_ref, sin_ref, h_ref, k_ref, v_ref, q_ref):
    width = x_ref.shape[1]
    x = x_ref[...].astype(F32)
    hidden = (x * rms_scale(x) * g_ref[...]).astype(BF)
    h_ref[...] = hidden
    copies = width // SLAB
    cos = jnp.concatenate([cos_ref[...]] * copies, axis=1)
    sin = jnp.concatenate([sin_ref[...]] * copies, axis=1)
    key = dot(hidden, w_ref[:, width : 2 * width])
    k_ref[...] = (key * cos + swap_halves(key) * sin).astype(BF)
    v_ref[...] = dot(hidden, w_ref[:, 2 * width : 3 * width]).astype(BF)

    @pl.when(pl.program_id(0) == 0)
    def _():
        query = dot(hidden, w_ref[:, :width])
        q_ref[...] = (query * cos + swap_halves(query) * sin).astype(BF)


def project(x_win, weights, gain, cos, sin, rows):
    total, width = x_win.shape
    return pl.pallas_call(
        project_kernel,
        grid=(total // rows,),
        in_specs=[
            pl.BlockSpec((rows, width), lambda i: (i, 0)),
            pl.BlockSpec((width, 3 * width), lambda i: (0, 0)),
            pl.BlockSpec((1, width), lambda i: (0, 0)),
            pl.BlockSpec((rows, SLAB), lambda i: (i, 0)),
            pl.BlockSpec((rows, SLAB), lambda i: (i, 0)),
        ],
        out_specs=[
            pl.BlockSpec((rows, width), lambda i: (i, 0)),
            pl.BlockSpec((rows, width), lambda i: (i, 0)),
            pl.BlockSpec((rows, width), lambda i: (i, 0)),
            pl.BlockSpec((rows, width), lambda i: (0, 0)),
        ],
        out_shape=[jax.ShapeDtypeStruct((total, width), BF)] * 3
        + [jax.ShapeDtypeStruct((rows, width), BF)],
        name="project",
    )(x_win, weights, gain, cos, sin)


def attend_kernel(
    near_ref, q_ref, k_ref, v_ref, sq_ref, sk_ref, o_ref, l_ref, s_buf, m_buf, d_buf, a_buf
):
    rows = q_ref.shape[0]
    slots = k_ref.shape[0] // rows
    scale = HEAD_DIM**-0.5
    seg_q = sq_ref[...]
    lane = lax.broadcasted_iota(jnp.int32, (rows, SLAB), 1)
    parts = []
    for head in range(2):
        query = q_ref[...] * head_mask(rows, head)
        m_buf[...] = jnp.full_like(m_buf, NEG_LARGE)
        d_buf[...] = jnp.zeros_like(d_buf)
        a_buf[...] = jnp.zeros_like(a_buf)
        for j in range(slots):

            @pl.when(near_ref[j] > 0)
            def _(j=j, query=query):
                scores = dot_nt(query, k_ref[j * rows : (j + 1) * rows, :]) * scale
                scores = jnp.where(seg_q == sk_ref[j], scores, NEG_LARGE)
                s_buf[j] = scores
                top = m_buf[...]
                for n in range(rows // SLAB):
                    top = jnp.maximum(top, scores[:, n * SLAB : (n + 1) * SLAB])
                m_buf[...] = top

        top = jnp.max(m_buf[...], axis=1, keepdims=True)
        for j in range(slots):

            @pl.when(near_ref[j] > 0)
            def _(j=j, top=top):
                probs = jnp.exp(s_buf[j] - top)
                total = d_buf[...]
                for n in range(rows // SLAB):
                    total = total + probs[:, n * SLAB : (n + 1) * SLAB]
                d_buf[...] = total
                a_buf[...] += dot(probs.astype(BF), v_ref[j * rows : (j + 1) * rows, :])

        total = jnp.sum(d_buf[...], axis=1, keepdims=True)
        parts.append((a_buf[...] / total, top + jnp.log(total)))
    first = lane < HEAD_DIM
    o_ref[...] = jnp.where(first, parts[0][0], parts[1][0])
    l_ref[...] = jnp.where(first, parts[0][1], parts[1][1])


def attend(near, q, k, v, seg_q, seg_k):
    rows, width = q.shape
    total = k.shape[0]
    slots = total // rows
    grid_spec = pltpu.PrefetchScalarGridSpec(
        num_scalar_prefetch=1,
        grid=(width // SLAB,),
        in_specs=[
            pl.BlockSpec((rows, SLAB), lambda i, n: (0, i)),
            pl.BlockSpec((total, SLAB), lambda i, n: (0, i)),
            pl.BlockSpec((total, SLAB), lambda i, n: (0, i)),
            pl.BlockSpec((rows, 1), lambda i, n: (0, 0)),
            pl.BlockSpec((slots, 1, rows), lambda i, n: (0, 0, 0)),
        ],
        out_specs=[
            pl.BlockSpec((rows, SLAB), lambda i, n: (0, i)),
            pl.BlockSpec((rows, SLAB), lambda i, n: (0, i)),
        ],
        scratch_shapes=[
            pltpu.VMEM((slots, rows, rows), F32),
            pltpu.VMEM((rows, SLAB), F32),
            pltpu.VMEM((rows, SLAB), F32),
            pltpu.VMEM((rows, SLAB), F32),
        ],
    )
    return pl.pallas_call(
        attend_kernel,
        grid_spec=grid_spec,
        out_shape=[jax.ShapeDtypeStruct((rows, width), F32)] * 2,
        name="attend",
    )(near, q, k, v, seg_q[:, None], seg_k.reshape(slots, 1, rows))


def attend_back_kernel(
    near_ref,
    q_ref,
    k_ref,
    v_ref,
    g_ref,
    o_ref,
    l_ref,
    sq_ref,
    sk_ref,
    cos_ref,
    sin_ref,
    dq_ref,
    dk_ref,
    dv_ref,
    acc,
):
    rows = q_ref.shape[0]
    slots = k_ref.shape[0] // rows
    scale = HEAD_DIM**-0.5
    grads = g_ref[...]
    masks = [head_mask(rows, head) for head in range(2)]
    q_cat = jnp.concatenate([q_ref[...] * m for m in masks], axis=0)
    g_cat = jnp.concatenate([grads * m for m in masks], axis=0)
    lse_t = jnp.transpose(l_ref[...])
    delta_t = jnp.transpose(grads.astype(F32) * o_ref[...])
    lse = jnp.concatenate([lse_t[:1], lse_t[HEAD_DIM : HEAD_DIM + 1]], axis=1)
    delta = jnp.concatenate(
        [
            jnp.sum(delta_t[:HEAD_DIM], axis=0, keepdims=True),
            jnp.sum(delta_t[HEAD_DIM:], axis=0, keepdims=True),
        ],
        axis=1,
    )
    seg_q = jnp.concatenate([sq_ref[...]] * 2, axis=1)
    acc[...] = jnp.zeros_like(acc)

    def turned(values, cos, sin):
        values = values * scale
        return (values * cos - swap_halves(values) * sin).astype(BF)

    for j in range(slots):
        part = slice(j * rows, (j + 1) * rows)

        @pl.when(near_ref[j] > 0)
        def _(part=part):
            keys = k_ref[part, :]
            scores = dot_nt(keys, q_cat) * scale
            probs = jnp.where(sk_ref[part, :] == seg_q, jnp.exp(scores - lse), 0.0)
            prob_grads = dot_nt(v_ref[part, :], g_cat)
            score_grads = (probs * (prob_grads - delta)).astype(BF)
            dk = dot(score_grads, q_cat)
            dk_ref[part, :] = turned(dk, cos_ref[part, :], sin_ref[part, :])
            dv_ref[part, :] = dot(probs.astype(BF), g_cat).astype(BF)
            acc[...] += dot_tn(score_grads[:, :rows], keys * masks[0]) + dot_tn(
                score_grads[:, rows:], keys * masks[1]
            )

        @pl.when(near_ref[j] <= 0)
        def _(part=part):
            dk_ref[part, :] = jnp.zeros((rows, SLAB), BF)
            dv_ref[part, :] = jnp.zeros((rows, SLAB), BF)

    dq_ref[...] = turned(acc[...], cos_ref[:rows, :], sin_ref[:rows, :])


def attend_back(near, q, k, v, grads, attended, lse, seg_q, seg_k, cos, sin):
    rows, width = q.shape
    total = k.shape[0]
    own = pl.BlockSpec((rows, SLAB), lambda i, n: (0, i))
    window = pl.BlockSpec((total, SLAB), lambda i, n: (0, i))
    table = pl.BlockSpec((total, SLAB), lambda i, n: (0, 0))
    grid_spec = pltpu.PrefetchScalarGridSpec(
        num_scalar_prefetch=1,
        grid=(width // SLAB,),
        in_specs=[
            own,
            window,
            window,
            own,
            own,
            own,
            pl.BlockSpec((1, rows), lambda i, n: (0, 0)),
            pl.BlockSpec((total, 1), lambda i, n: (0, 0)),
            table,
            table,
        ],
        out_specs=[own, window, window],
        scratch_shapes=[pltpu.VMEM((rows, SLAB), F32)],
    )
    return pl.pallas_call(
        attend_back_kernel,
        grid_spec=grid_spec,
        out_shape=[
            jax.ShapeDtypeStruct((rows, width), BF),
            jax.ShapeDtypeStruct((total, width), BF),
            jax.ShapeDtypeStruct((total, width), BF),
        ],
        name="attend_back",
    )(near, q, k, v, grads, attended, lse, seg_q[None, :], seg_k[:, None], cos, sin)


def shards(
    tokens,
    segment_ids,
    routes,
    norm1_gain,
    w_query,
    w_key,
    w_value,
    w_out,
    norm2_gain,
    w_router,
    shared_gate,
    shared_up,
    shared_down,
    expert_gate,
    expert_up,
    expert_down,
    out_grad,
):
    rows, width = tokens.shape
    reps = lax.axis_size("rep")
    group = lax.axis_size("ep")
    place = lax.axis_index("ep")
    pack_rows = rows * group
    top_count = routes.shape[1]
    experts = w_router.shape[1]
    capacity = 2 * rows * top_count // experts
    ff = shared_gate.shape[1]
    ff_part = ff // group
    ff_row = ff_part // reps
    pad = SLAB

    swap = [(i, i ^ 1) for i in range(group)]
    upward = [(i, i + 2) for i in range(group - 2)]
    downward = [(i + 2, i) for i in range(group - 2)]
    back = group // 4

    small = jnp.concatenate(
        [
            norm1_gain[:, None],
            norm2_gain[:, None],
            w_router,
            jnp.zeros((w_router.shape[0], pad - 2 - experts), BF),
        ],
        axis=1,
    )
    dense = lax.all_gather(
        jnp.concatenate([w_query, w_key, w_value, w_out, small], axis=1), ALL, axis=0, tiled=True
    )
    meta = lax.all_gather(
        jnp.concatenate([segment_ids.reshape(1, rows), routes.T], axis=0), "ep", axis=0
    )
    seg_all = meta[:, 0, :]
    slots = [tokens, lax.ppermute(tokens, "ep", swap)]
    current = tokens
    for _ in range(back):
        current = lax.ppermute(current, "ep", upward)
        slots += [current, lax.ppermute(current, "ep", swap)]
    x_win = jnp.concatenate(slots, axis=0)
    block_of_slot = jnp.stack(
        [base - 2 * k for k in range(back + 1) for base in (place, place ^ 1)]
    )
    seg_own = segment_ids.reshape(rows)
    usable = jnp.logical_and(block_of_slot >= 0, block_of_slot <= place)
    seg_win = jnp.where(usable[:, None], seg_all[jnp.clip(block_of_slot, 0, group - 1)], -1)
    near = (jnp.max(seg_win, axis=1) >= seg_own[0]).astype(jnp.int32)
    seg_win = seg_win.reshape(-1)

    half = HEAD_DIM // 2
    inverse = jnp.exp(jnp.arange(half).astype(F32) * (-2.0 * math.log(10000.0) / HEAD_DIM))
    places = (block_of_slot[:, None] * rows + jnp.arange(rows, dtype=jnp.int32)).reshape(-1)
    turned = places.astype(F32)[:, None] * inverse[None, :]
    cos, sin = jnp.cos(turned), jnp.sin(turned)
    cos = jnp.concatenate([cos] * 4, axis=1)
    sin = jnp.concatenate([-sin, sin] * 2, axis=1)

    grad_all = lax.all_gather(out_grad, "ep", axis=0, tiled=True)

    pieces = jnp.concatenate(
        [
            shared_gate.reshape(-1, reps, group, ff_row).transpose(2, 0, 1, 3).reshape(
                group, -1, ff_part
            ),
            shared_up.reshape(-1, reps, group, ff_row).transpose(2, 0, 1, 3).reshape(
                group, -1, ff_part
            ),
        ],
        axis=2,
    )
    pieces = lax.all_to_all(pieces, "ep", split_axis=0, concat_axis=0, tiled=True)
    shared_in = lax.all_gather(pieces, "rep", axis=0, tiled=True).reshape(width, 2 * ff_part)
    gate_part = shared_in[:, :ff_part]
    up_part = shared_in[:, ff_part:]
    down_part = lax.all_gather(shared_down, "rep", axis=0, tiled=True)

    gain_first = dense[:, 4 * width].astype(F32)[None, :]
    gain_second = dense[:, 4 * width + 1].astype(F32)[None, :]
    router = dense[:, 4 * width + 2 : 4 * width + 2 + experts]
    output_matrix = dense[:, 3 * width : 4 * width]
    hidden_win, k_win, v_win, queries = project(x_win, dense, gain_first, cos, sin, rows)
    attended, lse = attend(near, queries, k_win, v_win, seg_own, seg_win)
    attended_low = attended.astype(BF)
    layer_inputs = tokens.astype(F32)
    middle = layer_inputs + dot(attended_low, output_matrix)
    scale_second = rms_scale(middle)
    normed_second = middle * scale_second
    hidden_second = (normed_second * gain_second).astype(BF)

    hidden_all = lax.all_gather(hidden_second, "ep", axis=0, tiled=True)

    chosen = jnp.any(meta[:, 1:, :] == place, axis=1)
    chosen_low = chosen.astype(BF)
    before = (
        lax.broadcasted_iota(jnp.int32, (rows, rows), 0)
        < lax.broadcasted_iota(jnp.int32, (rows, rows), 1)
    ).astype(BF)
    rank = dot(chosen_low, before)
    picker = jnp.where(
        jnp.logical_and(
            chosen[:, None, :],
            rank[:, None, :] == jnp.arange(capacity, dtype=jnp.int32).astype(F32)[None, :, None],
        ),
        1.0,
        0.0,
    ).astype(BF)

    def pick(values):
        return lax.dot_general(
            picker,
            values.reshape(group, rows, -1),
            (((2,), (1,)), ((0,), (0,))),
            preferred_element_type=F32,
        ).reshape(group * capacity, -1)

    def unpick(values):
        return lax.dot_general(
            picker,
            values.reshape(group, capacity, -1),
            (((1,), (1,)), ((0,), (0,))),
            preferred_element_type=F32,
        ).reshape(pack_rows, -1)

    gate_matrix, up_matrix, down_matrix = expert_gate[0], expert_up[0], expert_down[0]
    grads_in = pick(grad_all).astype(BF)
    hidden_grad_raw = dot_nt(grads_in, down_matrix)
    shared_hidden_grad = dot_nt(grad_all, down_part)

    logits = dot(hidden_all, router)
    shifted = jnp.exp(logits - jnp.max(logits, axis=1, keepdims=True))
    router_probs = shifted / jnp.sum(shifted, axis=1, keepdims=True)
    own_column = lax.broadcasted_iota(jnp.int32, (1, experts), 1) == place
    own_prob = jnp.sum(jnp.where(own_column, router_probs, 0.0), axis=1, keepdims=True)
    own_gate = own_prob.reshape(group, 1, rows)
    gate_slot = jnp.sum(picker.astype(F32) * own_gate, axis=2).reshape(group * capacity, 1)

    received = pick(hidden_all).astype(BF)
    gate_pre = dot(received, gate_matrix)
    up_pre = dot(received, up_matrix)
    logistic = jax.nn.sigmoid(gate_pre)
    silu = gate_pre * logistic
    slope = logistic * (1.0 + gate_pre * (1.0 - logistic))
    expert_hidden = (silu * up_pre).astype(BF)
    expert_result = dot(expert_hidden, down_matrix).astype(BF).astype(F32)
    hidden_grad = gate_slot * hidden_grad_raw
    gate_pre_grad = (hidden_grad * up_pre * slope).astype(BF)
    up_pre_grad = (hidden_grad * silu).astype(BF)
    row_grads = (dot_nt(gate_pre_grad, gate_matrix) + dot_nt(up_pre_grad, up_matrix)).astype(BF)
    grads_f32 = grads_in.astype(F32)
    gate_grad = jnp.sum(grads_f32 * expert_result, axis=1).reshape(group, capacity, 1)
    prob_grad = jnp.sum(picker.astype(F32) * gate_grad, axis=1).reshape(pack_rows, 1)
    logit_part = (
        prob_grad * own_prob * (jnp.where(own_column, 1.0, 0.0) - router_probs)
    ).astype(BF)
    choice_grad = (gate_slot * grads_f32).astype(BF)

    shared_pre = dot(hidden_all, gate_part)
    shared_lin = dot(hidden_all, up_part)
    shared_logistic = jax.nn.sigmoid(shared_pre)
    shared_silu = shared_pre * shared_logistic
    shared_slope = shared_logistic * (1.0 + shared_pre * (1.0 - shared_logistic))
    shared_hidden = (shared_silu * shared_lin).astype(BF)
    shared_pre_grad = (shared_hidden_grad * shared_lin * shared_slope).astype(BF)
    shared_lin_grad = (shared_hidden_grad * shared_silu).astype(BF)

    second_part = (
        unpick(row_grads)
        + dot_nt(shared_pre_grad, gate_part)
        + dot_nt(shared_lin_grad, up_part)
        + dot_nt(logit_part, router)
    )
    second_grad = lax.psum_scatter(
        second_part.astype(BF), "ep", scatter_dimension=0, tiled=True
    ).astype(F32)
    out_part = unpick((gate_slot * expert_result).astype(BF)) + dot(shared_hidden, down_part)
    out_sum = lax.psum_scatter(
        out_part.astype(BF), "ep", scatter_dimension=0, tiled=True
    ).astype(F32)
    layer_out = (middle + out_sum).astype(BF)

    def over_reps(term):
        return lax.psum_scatter(term.astype(BF), "rep", scatter_dimension=0, tiled=True).astype(
            F32
        )

    expert_gate_grad = over_reps(dot_tn(gate_pre_grad, received)).T[None]
    expert_up_grad = over_reps(dot_tn(up_pre_grad, received)).T[None]
    expert_down_grad = over_reps(dot_tn(choice_grad, expert_hidden)).T[None]

    gate_term = dot_tn(hidden_all, shared_pre_grad)
    up_term = dot_tn(hidden_all, shared_lin_grad)
    down_term = dot_tn(shared_hidden, grad_all)
    stacked = jnp.concatenate(
        [
            gate_term.astype(BF).reshape(reps, width // reps, ff_part),
            up_term.astype(BF).reshape(reps, width // reps, ff_part),
        ],
        axis=2,
    )
    stacked = lax.psum_scatter(stacked, "rep", scatter_dimension=0, tiled=True)
    shared_down_grad = over_reps(down_term)
    stacked = lax.all_to_all(
        stacked.reshape(group, -1, 2 * ff_part), "ep", split_axis=0, concat_axis=0, tiled=True
    ).astype(F32)

    def columns(term):
        return (
            term.reshape(group, -1, reps, ff_row).transpose(1, 2, 0, 3).reshape(-1, ff)
        )

    shared_gate_grad = columns(stacked[:, :, :ff_part])
    shared_up_grad = columns(stacked[:, :, ff_part:])

    grad_output = out_grad.astype(F32)
    grad_normed = second_grad * gain_second
    middle_grad = grad_output + scale_second * (
        grad_normed
        - normed_second * jnp.mean(grad_normed * normed_second, axis=1, keepdims=True)
    )
    gain_second_term = jnp.sum(second_grad * normed_second, axis=0)
    attn_grad = middle_grad.astype(BF)
    attended_grad = dot_nt(attn_grad, output_matrix).astype(BF)

    def over_all(term):
        columns_in = term.shape[1]
        term = term.astype(BF).reshape(reps, group, -1, columns_in).transpose(1, 0, 2, 3)
        term = lax.psum_scatter(term, "ep", scatter_dimension=0, tiled=False)
        return lax.psum_scatter(term, "rep", scatter_dimension=0, tiled=False).astype(F32)

    early = over_all(
        jnp.concatenate(
            [
                dot_tn(attended_low, attn_grad),
                dot_tn(hidden_all, logit_part),
                gain_second_term[:, None],
                jnp.zeros((width, pad - 1 - experts), F32),
            ],
            axis=1,
        )
    )

    dq, dk_win, dv_win = attend_back(
        near, queries, k_win, v_win, attended_grad, attended, lse, seg_own, seg_win, cos, sin
    )
    query_matrix = dense[:, :width]
    key_matrix = dense[:, width : 2 * width]
    value_matrix = dense[:, 2 * width : 3 * width]
    first_part = dot_nt(dk_win, key_matrix) + dot_nt(dv_win, value_matrix)
    first_own = dot_nt(dq, query_matrix)
    x_f32 = x_win.astype(F32)
    normed_win = x_f32 * rms_scale(x_f32)
    normed_first = normed_win[:rows]
    scale_first = rms_scale(layer_inputs)
    gain_first_term = jnp.sum(first_part * normed_win, axis=0) + jnp.sum(
        first_own * normed_first, axis=0
    )
    by_slot = first_part.reshape(back + 1, 2, rows, width)
    given = lax.ppermute(by_slot[:, 1].astype(BF), "ep", swap).astype(F32)
    sums = by_slot[:, 0] + given
    first_grad = sums[back]
    for k in range(back - 1, -1, -1):
        first_grad = sums[k] + lax.ppermute(first_grad.astype(BF), "ep", downward).astype(F32)
    first_grad = first_grad + first_own
    grad_normed = first_grad * gain_first
    tokens_grad = middle_grad + scale_first * (
        grad_normed - normed_first * jnp.mean(grad_normed * normed_first, axis=1, keepdims=True)
    )
    late = over_all(
        jnp.concatenate(
            [
                dot_tn(hidden_win[:rows], dq),
                dot_tn(hidden_win, dk_win),
                dot_tn(hidden_win, dv_win),
                gain_first_term[:, None],
                jnp.zeros((width, pad - 1), F32),
            ],
            axis=1,
        )
    )
    return (
        layer_out,
        tokens_grad,
        late[:, 3 * width],
        late[:, :width],
        late[:, width : 2 * width],
        late[:, 2 * width : 3 * width],
        early[:, :width],
        early[:, width + experts],
        early[:, width : width + experts],
        shared_gate_grad,
        shared_up_grad,
        shared_down_grad,
        expert_gate_grad,
        expert_up_grad,
        expert_down_grad,
    )


def solution(mesh):
    row = P(ALL, None)
    expert = P("ep", None, None)
    expert_out = P("ep", None, "rep")
    return jax.shard_map(
        shards,
        mesh=mesh,
        in_specs=(
            row,
            P("rep", "ep"),
            row,
            P(ALL),
            row,
            row,
            row,
            row,
            P(ALL),
            row,
            row,
            row,
            row,
            expert,
            expert,
            expert,
            row,
        ),
        out_specs=(
            row,
            row,
            P(ALL),
            row,
            row,
            row,
            row,
            P(ALL),
            row,
            row,
            row,
            row,
            expert_out,
            expert_out,
            expert_out,
        ),
        check_vma=False,
    )
```

time: 1680 us -> 667 us (0.40)
  waiting for transfers between devices: 1100 us -> 309 us
  blocking collectives: 132 us -> 40.5 us
  matrix products: 209 us -> 124 us
  local copies, waits for them, and re-layouts: 126 us -> 52.3 us
  Pallas kernels: 0 us -> 32.9 us
  starting transfers between devices: 18.2 us -> 48.5 us
  other arithmetic: 67.8 us -> 39.1 us
    reduce_scatter x10 -> x8, waiting for transfers between devices: 819 us -> 211 us  [the longest x4 100 us: over_reps(): lax.psum_scatter(term.astype(BF), 'rep', scatter_dimension=0, tiled=True)]
    all_to_all x4 -> x2, waiting for transfers between devices: 122 us -> 8.58 us  [the longest x1 6.47 us: shards(): lax.all_to_all(stacked.reshape(group, -1, 2 * ff_part), 'ep', split_axis=...]
    all_gather x9 -> x3, waiting for transfers between devices: 119 us -> 13.1 us  [the longest x1 13.1 us: shards(): lax.all_gather(jnp.concatenate([w_query, w_key, w_value, w_out, small], a...]
    dot_general x61 -> x35, matrix products: 209 us -> 124 us  [the longest x11 53 us: dot_nt(): lax.dot_general(a, b, (((1,), (1,)), ((), ())), preferred_element_type=F32)]
    unnamed x2 -> x0, blocking collectives: 82.3 us -> none
    ppermute x0 -> x8, waiting for transfers between devices: none -> 34.4 us  [the longest x2 25.7 us: shards(): lax.ppermute(first_grad.astype(BF), 'ep', downward).astype(F32)]
    pallas_call x0 -> x3, Pallas kernels: none -> 32.9 us  [the longest x1 11.1 us: project(): pl.pallas_call(project_kernel, grid=(total // rows,), in_specs=[pl.BlockS...]
    dynamic_slice x24 -> x0, local copies, waits for them, and re-layouts: 29.1 us -> none  [the longest x4 9.65 us: inner_step(): lax.dynamic_slice_in_dim(value_piece, offset, inner_rows, 0)]
  transfers between devices with their start and end apart: 24 -> 24, of which waited for: 18 -> 15; matrix products, arithmetic and copies ran while one was open for 18% -> 20% of each run, Pallas kernels for 0% -> 5%
where the time goes in v1:
time: 667 us; the launch traced here: 661 us
  waiting for transfers between devices  309 us (46%)
  matrix products  124 us (19%)
  local copies, waits for them, and re-layouts  52.3 us (8%)
  starting transfers between devices  48.5 us (7%)
  blocking collectives  40.5 us (6%)
  other arithmetic  39.1 us (6%)
  Pallas kernels  32.9 us (5%)
  between operations  15.1 us (2%)
    reduce_scatter x4, waiting for transfers between devices, over_reps(): lax.psum_scatter(term.astype(BF), 'rep', scatter_dimension=0, tiled=True)  100 us
    dot_general x11, matrix products, dot_nt(): lax.dot_general(a, b, (((1,), (1,)), ((), ())), preferred_element_type=F32)  53 us
    reduce_scatter x2, waiting for transfers between devices, over_all(): term = lax.psum_scatter(term, 'ep', scatter_dimension=0, tiled=False)  46.7 us
    unnamed x17, waiting for transfers between devices  41.7 us
    reduce_scatter x1, waiting for transfers between devices, shards(): lax.psum_scatter(out_part.astype(BF), 'ep', scatter_dimension=0, tiled=True)  40.2 us
    dot_general x11, matrix products, dot_tn(): lax.dot_general(a, b, (((0,), (0,)), ((), ())), preferred_element_type=F32)  35.4 us
    dot_general x9, matrix products, dot(): lax.dot_general(a, b, (((1,), (0,)), ((), ())), preferred_element_type=F32)  25.8 us
    ppermute x2, waiting for transfers between devices, shards(): lax.ppermute(first_grad.astype(BF), 'ep', downward).astype(F32)  25.7 us
  transfers between devices with their start and end apart: 24, of which 15 were waited for; matrix products, arithmetic and copies ran while one was open for 20% of the time, Pallas kernels for 5%

profile of v1, /device:TPU:0, one launch (start us, length us, event | category | flops | bytes accessed | tf_op | source)
XLA Modules:
  0.0 661.1 jit_solution(14844590081710121184)
XLA Ops:
  12.1 5.7 collective-permute-start.1
  18.7 17.4 %all-gather.1 = s32[8,3,256]{2,1,0:T(4,128)S(1)} all-gather(s32[1,3,256]{2,1,0:T(4,128)S(1)} %add_bitcast_fusion), channel_id=2, replica_groups=mesh['rep'=4,'ep'=8] {'ep'}, dimensions={0}, use_global_device_ids=true | all-gather | bytes 27648 | tf_op jit(solution)/shard_map/all_gather | solution.py:323
  37.5 2.8 fusion.85
  43.5 4.4 collective-permute-start.3
  52.0 5.9 collective-permute-done.3
  65.9 13.1 %all-gather.6.cloned.1.call-done.w_ref = bf16[768,3200]{1,0:T(8,128)(2,1)} async-done(((bf16[24,3200]{1,0:T(8,128)(2,1)}), bf16[768,3200]{1,0:T(8,128)(2,1)}) %all-gather.6.cloned.1.call-update) | async-done | bytes 4915216 | tf_op jit(solution)/shard_map/all_gather | solution.py:320
  81.5 11.1 %project.1 = (bf16[1536,768]{1,0:T(8,128)(2,1)}, bf16[1536,768]{1,0:T(8,128)(2,1)}, bf16[1536,768]{1,0:T(8,128)(2,1)}, bf16[256,768]{1,0:T(8,128)(2,1)}) custom-call(bf16[1536,768]{1,0:T(8,128)(2,1)} %constant_dynamic-update-slice_fusion.x_ref, bf16[768,3200]{1,0:T(8,128)(2,1)} %all-gather.6.cloned.1.call-done.w_ref, f32[1,768]{1,0:T(1,128)} %reshape.549.g_ref, ...), custom_call_target="tpu_custom_call" | custom-call | tf_op jit(solution)/shard_map/project/pallas_call | solution.py:72
  92.5 10.9 %attend.1 = (f32[256,768]{1,0:T(8,128)}, f32[256,768]{1,0:T(8,128)}) custom-call(s32[6]{0:T(128)} %compare_convert_fusion.near_ref, bf16[256,768]{1,0:T(8,128)(2,1)} %get-tuple-element.24.q_ref, bf16[1536,768]{1,0:T(8,128)(2,1)} %get-tuple-element.25.k_ref, bf16[1536,768]{1,0:T(8,128)(2,1)} %get-tuple-element.26.v_ref, s32[256,1]{1,0:T(8,128)} %copy.168.sq_ref, ...), custom_call_target="tpu_custom_call" | custom-call | tf_op jit(solution)/shard_map/attend/pallas_call | solution.py:164
  112.3 19.9 %all-to-all-start = ((bf16[8,24,512]{2,1,0:T(8,128)(2,1)}), bf16[8,24,512]{2,1,0:T(8,128)(2,1)}, u32[]{:S(2)}, u32[]{:S(2)}) async-start(bf16[8,24,512]{2,1,0:T(8,128)(2,1)} %pad_maximum_fusion.3), calls=%async_computation | async-start | bytes 393216 | tf_op jit(solution)/shard_map/all_to_all | solution.py:363
  133.3 10.0 %all_gather.26 = bf16[256,768]{1,0:T(8,128)(2,1)S(1)} all-gather(bf16[64,768]{1,0:T(8,128)(2,1)} %param.29), channel_id=1, replica_groups=mesh['rep'=4,'ep'=8] {'rep'}, dimensions={0}, use_global_device_ids=true | all-gather | bytes 491520 | tf_op jit(solution)/shard_map/all_gather | solution.py:367
  146.4 13.0 %all_gather.25 = bf16[32,24,512]{2,1,0:T(8,128)(2,1)} all-gather(bf16[8,24,512]{2,1,0:T(8,128)(2,1)} %all-to-all-done), channel_id=1, replica_groups=mesh['rep'=4,'ep'=8] {'rep'}, dimensions={0}, use_global_device_ids=true | all-gather | bytes 983040 | tf_op jit(solution)/shard_map/all_gather | solution.py:364
  159.4 4.4 convolution_convert_fusion.3
  166.2 2.9 fusion.106
  172.3 3.3 convolution_convert_fusion.4
  175.6 3.4 fusion.19
  179.1 6.2 multiply_convert_fusion.2
  185.3 4.7 fusion.7
  191.4 21.5 %multiply_convert_fusion.1 = (bf16[1024,2048]{1,0:T(8,128)(2,1)}, bf16[1024,2048]{1,0:T(8,128)(2,1)}) fusion(f32[1024,2048]{1,0:T(8,128)} %copy-done.62, f32[1024,2048]{1,0:T(8,128)} %get-tuple-element.168, f32[1024]{0:T(1024)S(1)} %bitcast.225, bf16[1024,768]{1,0:T(8,128)(2,1)S(1)} %bitcast.209, bf16[1,2048,768]{2,1,0:T(8,128)(2,1)S(1)} %copy-done), kind=kOutput, calls=%fused_computation.2 | convolution fusion | flops 3250585600 | bytes 29888512 | tf_op jit(solution)/shard_map/dot_general | solution.py:25
  212.9 5.5 fusion.13
  218.4 3.5 add_convert_fusion
  225.6 2.7 multiply_convert_fusion.4
  230.7 4.0 fusion.3
  238.3 2.6 fusion.4
  246.4 4.1 convolution_convert_fusion.9
  250.6 24.2 %reduce-scatter.20.cloned.1.call-done = bf16[256,768]{1,0:T(8,128)(2,1)} async-done(((bf16[2048,768]{1,0:T(8,128)(2,1)}), bf16[256,768]{1,0:T(8,128)(2,1)}) %reduce-scatter.20.cloned.1.call-update) | async-done | bytes 393232 | tf_op jit(solution)/shard_map/reduce_scatter | solution.py:464
  276.6 40.2 %reduce-scatter.18.cloned.1.call-done = bf16[256,768]{1,0:T(8,128)(2,1)} async-done(((bf16[2048,768]{1,0:T(8,128)(2,1)}), bf16[256,768]{1,0:T(8,128)(2,1)}) %reduce-scatter.18.cloned.1.call-update) | async-done | bytes 393232 | tf_op jit(solution)/shard_map/reduce_scatter | solution.py:468
  321.1 7.2 %convolution_convert_fusion = bf16[768,2048]{1,0:T(8,128)(2,1)} fusion(bf16[1024,2048]{1,0:T(8,128)(2,1)} %copy-done.61, bf16[1024,768]{1,0:T(8,128)(2,1)S(1)} %bitcast.210, f32[1024]{0:T(1024)S(1)} %bitcast.227), kind=kOutput, calls=%fused_computation.20 | convolution fusion | flops 3225157632 | bytes 8916992 | tf_op jit(solution)/shard_map/dot_general | solution.py:29
  329.7 7.5 %convolution_convert_fusion.2 = bf16[2048,768]{1,0:T(8,128)(2,1)} fusion(bf16[1024,2048]{1,0:T(8,128)(2,1)} %get-tuple-element.146, bf16[1024,768]{1,0:T(8,128)(2,1)S(1)} %bitcast.207), kind=kOutput, calls=%fused_computation.22 | convolution fusion | flops 3222798336 | bytes 8912896 | tf_op jit(solution)/shard_map/dot_general | solution.py:29
  341.4 2.5 convolution_convert_fusion.12.g_ref
  344.0 10.9 %attend_back.1 = (bf16[256,768]{1,0:T(8,128)(2,1)}, bf16[1536,768]{1,0:T(8,128)(2,1)}, bf16[1536,768]{1,0:T(8,128)(2,1)}) custom-call(s32[6]{0:T(128)} %compare_convert_fusion.near_ref, bf16[256,768]{1,0:T(8,128)(2,1)} %get-tuple-element.24.q_ref, bf16[1536,768]{1,0:T(8,128)(2,1)} %get-tuple-element.25.k_ref, bf16[1536,768]{1,0:T(8,128)(2,1)} %get-tuple-element.26.v_ref, ...), custom_call_target="tpu_custom_call" | custom-call | tf_op jit(solution)/shard_map/attend_back/pallas_call | solution.py:262
  354.9 4.2 fusion.34
  359.2 4.6 multiply_reduce_fusion
  364.1 2.7 collective-permute-done.5
  370.6 11.4 %collective-permute-done.6 = bf16[256,768]{1,0:T(8,128)(2,1)S(1)} collective-permute-done((bf16[256,768]{1,0:T(8,128)(2,1)S(1)}, bf16[256,768]{1,0:T(8,128)(2,1)S(1)}, u32[]{:S(2)}, u32[]{:S(2)}) %collective-permute-start.6) | collective-permute-done | bytes 393248 | tf_op jit(solution)/shard_map/ppermute | solution.py:554
  389.6 14.4 %collective-permute-done.7 = bf16[256,768]{1,0:T(8,128)(2,1)S(1)} collective-permute-done((bf16[256,768]{1,0:T(8,128)(2,1)S(1)}, bf16[256,768]{1,0:T(8,128)(2,1)S(1)}, u32[]{:S(2)}, u32[]{:S(2)}) %collective-permute-start.7) | collective-permute-done | bytes 393248 | tf_op jit(solution)/shard_map/ppermute | solution.py:554
  404.0 2.7 multiply_reduce_fusion.1
  407.2 6.7 %concatenate.70 = bf16[4,8,24,2432]{3,2,0,1:T(8,128)(2,1)} concatenate(bf16[4,8,24,768]{3,2,0,1:T(8,128)(2,1)} %copy.176, bf16[4,8,24,768]{3,2,0,1:T(8,128)(2,1)} %copy.177, bf16[4,8,24,768]{3,2,0,1:T(8,128)(2,1)} %copy.178, bf16[4,8,24,1]{3,2,0,1:T(8,128)(2,1)S(1)} %copy.179, bf16[4,8,24,127]{3,2,0,1:T(8,128)(2,1)S(1)} %broadcast_in_dim.111), dimensions={3} | concatenate | bytes 7471104 | tf_op jit(solution)/shard_map/concatenate | solution.py:561
  415.3 7.4 %convolution_convert_fusion.1 = bf16[2048,768]{1,0:T(8,128)(2,1)} fusion(bf16[1024,2048]{1,0:T(8,128)(2,1)} %get-tuple-element.147, bf16[1024,768]{1,0:T(8,128)(2,1)S(1)} %bitcast.208), kind=kOutput, calls=%fused_computation.21 | convolution fusion | flops 3222798336 | bytes 8912896 | tf_op jit(solution)/shard_map/dot_general | solution.py:29
  422.8 14.3 %all-to-all-start.1 = ((bf16[8,24,512]{2,1,0:T(8,128)(2,1)}), bf16[8,24,512]{2,1,0:T(8,128)(2,1)S(1)}, u32[]{:S(2)}, u32[]{:S(2)}) async-start(bf16[8,24,512]{2,1,0:T(8,128)(2,1)} %bitcast.220), calls=%async_computation.5 | async-start | bytes 393216 | tf_op jit(solution)/shard_map/all_to_all | solution.py:494
  438.9 6.5 all-to-all-done.1
  448.0 10.6 %reduce-scatter.32.cloned.1.call-done = bf16[192,2048]{1,0:T(8,128)(2,1)} async-done(((bf16[768,2048]{1,0:T(8,128)(2,1)}), bf16[192,2048]{1,0:T(8,128)(2,1)}) %reduce-scatter.32.cloned.1.call-update) | async-done | bytes 786448 | tf_op jit(solution)/shard_map/reduce_scatter | solution.py:474
  461.0 44.3 %reduce-scatter.28.cloned.1.call-done = bf16[512,768]{1,0:T(8,128)(2,1)} async-done(((bf16[2048,768]{1,0:T(8,128)(2,1)}), bf16[512,768]{1,0:T(8,128)(2,1)}) %reduce-scatter.28.cloned.1.call-update) | async-done | bytes 786448 | tf_op jit(solution)/shard_map/reduce_scatter | solution.py:474
  506.5 46.7 %reduce-scatter.22.cloned.1.call-done = bf16[1,4,24,2432]{3,2,1,0:T(8,128)(2,1)} async-done(((bf16[8,4,24,2432]{3,2,1,0:T(8,128)(2,1)}), bf16[1,4,24,2432]{3,2,1,0:T(8,128)(2,1)}) %reduce-scatter.22.cloned.1.call-update) | async-done | bytes 466960 | tf_op jit(solution)/shard_map/reduce_scatter | solution.py:519
  553.3 45.1 %reduce-scatter.30.cloned.1.call-done = bf16[512,768]{1,0:T(8,128)(2,1)} async-done(((bf16[2048,768]{1,0:T(8,128)(2,1)}), bf16[512,768]{1,0:T(8,128)(2,1)}) %reduce-scatter.30.cloned.1.call-update) | async-done | bytes 786448 | tf_op jit(solution)/shard_map/reduce_scatter | solution.py:474
  602.4 3.2 copy.187
  605.6 3.0 multiply_add_fusion
  608.5 16.3 %reduce-scatter.36.cloned.1.call-done = bf16[1,24,896]{2,1,0:T(8,128)(2,1)} async-done(((bf16[4,24,896]{2,1,0:T(8,128)(2,1)}), bf16[1,24,896]{2,1,0:T(8,128)(2,1)}) %reduce-scatter.36.cloned.1.call-update) | async-done | bytes 43024
  627.6 24.5 %reduce-scatter.34.cloned.1.call-done = bf16[1,24,2432]{2,1,0:T(8,128)(2,1)} async-done(((bf16[4,24,2432]{2,1,0:T(8,128)(2,1)}), bf16[1,24,2432]{2,1,0:T(8,128)(2,1)}) %reduce-scatter.34.cloned.1.call-update) | async-done | bytes 116752
  (288 shorter events, 101.8 us)
Async XLA Ops:
  7.2 178.1 %copy-start = (bf16[1,2048,768]{2,1,0:T(8,128)(2,1)S(1)}, bf16[1,2048,768]{2,1,0:T(8,128)(2,1)}, u32[]{:S(2)}) copy-start(bf16[1,2048,768]{2,1,0:T(8,128)(2,1)} %param.32) | copy-start | bytes 9437188
  7.2 71.8 %all-gather.6.cloned.1.call-start = ((), (), s32[]{:S(2)}) async-start(), calls=%async_computation.13 | async-start | bytes 5068800 | tf_op jit(solution)/shard_map/all_gather | solution.py:320
  11.3 148.2 %all-gather.10.cloned.1.call-start = ((), (), s32[]{:S(2)}) async-start(), calls=%async_computation.16 | async-start | bytes 3538944 | tf_op jit(solution)/shard_map/all_gather | solution.py:350
  12.0 154.2 %all-gather.8.cloned.1.call-start = ((), (), s32[]{:S(2)}) async-start(), calls=%async_computation.14 | async-start | bytes 3538944 | tf_op jit(solution)/shard_map/all_gather | solution.py:382
  12.1 31.5 %collective-permute-start.1 = (bf16[256,768]{1,0:T(8,128)(2,1)}, bf16[256,768]{1,0:T(8,128)(2,1)}, u32[]{:S(2)}, u32[]{:S(2)}) collective-permute-start(bf16[256,768]{1,0:T(8,128)(2,1)} %param.17), channel_id=1, source_target_pairs={{0,2},{1,3},{2,4},{3,5},{4,6},{5,7},{8,10},{9,11},{10,12},{11,13},... | collective-permute-start | bytes 1179656 | tf_op jit(solution)/shard_map/ppermute | solution.py:330
  17.8 40.1 %collective-permute-start = (bf16[256,768]{1,0:T(8,128)(2,1)}, bf16[256,768]{1,0:T(8,128)(2,1)}, u32[]{:S(2)}, u32[]{:S(2)}) collective-permute-start(bf16[256,768]{1,0:T(8,128)(2,1)} %param.17), channel_id=1, source_target_pairs={{0,1},{1,0},{2,3},{3,2},{4,5},{5,4},{6,7},{7,6},{8,9},{9,8},{10,11... | collective-permute-start | bytes 1179656 | tf_op jit(solution)/shard_map/ppermute | solution.py:327
  37.5 11.1 %copy-start.53 = (s32[1,256]{1,0:T(1,128)S(1)}, s32[1,256]{1,0:T(1,128)}, u32[]{:S(2)}) copy-start(s32[1,256]{1,0:T(1,128)} %sq_ref.1) | copy-start | bytes 3076
  37.5 13.7 %copy-start.12 = (bf16[256,768]{1,0:T(8,128)(2,1)S(1)}, bf16[256,768]{1,0:T(8,128)(2,1)}, u32[]{:S(2)}) copy-start(bf16[256,768]{1,0:T(8,128)(2,1)} %param.17) | copy-start | bytes 1179652
  40.3 10.1 %copy-start.54 = (s32[1,256]{1,0:T(1,128)S(1)}, s32[1,256]{1,0:T(1,128)}, u32[]{:S(2)}) copy-start(s32[1,256]{1,0:T(1,128)} %sq_ref.1) | copy-start | bytes 3076
  43.5 14.4 %collective-permute-start.3 = (bf16[256,768]{1,0:T(8,128)(2,1)}, bf16[256,768]{1,0:T(8,128)(2,1)}, u32[]{:S(2)}, u32[]{:S(2)}) collective-permute-start(bf16[256,768]{1,0:T(8,128)(2,1)} %collective-permute-done.1), channel_id=1, source_target_pairs={{0,2},{1,3},{2,4},{3,5},{4,6},{5,7},{8,10},{9,11},{10,12},{11,13},... | collective-permute-start | bytes 1179656 | tf_op jit(solution)/shard_map/ppermute | solution.py:330
  49.1 12.4 %collective-permute-start.2 = (bf16[256,768]{1,0:T(8,128)(2,1)}, bf16[256,768]{1,0:T(8,128)(2,1)}, u32[]{:S(2)}, u32[]{:S(2)}) collective-permute-start(bf16[256,768]{1,0:T(8,128)(2,1)} %collective-permute-done.1), channel_id=1, source_target_pairs={{0,1},{1,0},{2,3},{3,2},{4,5},{5,4},{6,7},{7,6},{8,9},{9,8},{10,11... | collective-permute-start | bytes 1179656 | tf_op jit(solution)/shard_map/ppermute | solution.py:331
  57.9 7.2 %collective-permute-start.4 = (bf16[256,768]{1,0:T(8,128)(2,1)}, bf16[256,768]{1,0:T(8,128)(2,1)S(1)}, u32[]{:S(2)}, u32[]{:S(2)}) collective-permute-start(bf16[256,768]{1,0:T(8,128)(2,1)} %collective-permute-done.3), channel_id=1, source_target_pairs={{0,1},{1,0},{2,3},{3,2},{4,5},{5,4},{6,7},{7,6},{8,9},{9,8},{10,11... | collective-permute-start | bytes 1179656 | tf_op jit(solution)/shard_map/ppermute | solution.py:331
  80.3 25.3 %copy-start.39 = (f32[768]{0:T(1024)}, f32[768]{0:T(1024)S(1)}, u32[]{:S(2)}) copy-start(f32[768]{0:T(1024)S(1)} %get-tuple-element.140) | copy-start | bytes 9220
  112.3 34.0 %all-to-all-start = ((bf16[8,24,512]{2,1,0:T(8,128)(2,1)}), bf16[8,24,512]{2,1,0:T(8,128)(2,1)}, u32[]{:S(2)}, u32[]{:S(2)}) async-start(bf16[8,24,512]{2,1,0:T(8,128)(2,1)} %pad_maximum_fusion.3), calls=%async_computation | async-start | bytes 393216 | tf_op jit(solution)/shard_map/all_to_all | solution.py:363
  132.3 142.6 %reduce-scatter.20.cloned.1.call-start = ((), (), s32[]{:S(2)}) async-start(), calls=%async_computation.17 | async-start | bytes 3538944 | tf_op jit(solution)/shard_map/reduce_scatter | solution.py:464
  132.8 31.0 %copy-start.50 = (f32[128]{0:T(128)}, f32[128]{0:T(128)S(1)}, u32[]{:S(2)}) copy-start(f32[128]{0:T(128)S(1)} %iota_convert_fusion) | copy-start | bytes 1540
  144.1 22.1 %copy-start.36 = (pred[8,256]{1,0:T(8,128)(4,1)}, pred[8,256]{1,0:T(8,128)(4,1)S(1)}, u32[]{:S(2)}) copy-start(pred[8,256]{1,0:T(8,128)(4,1)S(1)} %compare_reduce_fusion) | copy-start | bytes 6148
  179.1 6.2 copy-start.62
  179.1 6.2 copy-start.24
  185.3 6.1 copy-start.35
  191.4 21.5 %copy-start.46 = (f32[8,128]{1,0:T(8,128)}, f32[8,128]{1,0:T(8,128)S(1)}, u32[]{:S(2)}) copy-start(f32[8,128]{1,0:T(8,128)S(1)} %get-tuple-element.145) | copy-start | bytes 12292
  191.4 39.3 %copy-start.33 = (f32[2048]{0:T(1024)}, f32[2048]{0:T(1024)S(1)}, u32[]{:S(2)}) copy-start(f32[2048]{0:T(1024)S(1)} %mul.265) | copy-start | bytes 24580
  234.8 82.0 %reduce-scatter.18.cloned.1.call-start = ((), (), s32[]{:S(2)}) async-start(), calls=%async_computation.15 | async-start | bytes 3538944 | tf_op jit(solution)/shard_map/reduce_scatter | solution.py:468
  240.9 181.8 %reduce-scatter.38.cloned.1.call-start = ((), (), s32[]{:S(2)}) async-start(), calls=%async_computation.26 | async-start | bytes 983040
  245.4 191.9 %reduce-scatter.26.cloned.1.call-start = ((), (), s32[]{:S(2)}) async-start(), calls=%async_computation.20 | async-start | bytes 491520 | tf_op jit(solution)/shard_map/reduce_scatter | solution.py:474
  246.2 28.6 %copy-start.6 = (f32[256,768]{1,0:T(8,128)S(1)}, f32[256,768]{1,0:T(8,128)}, u32[]{:S(2)}) copy-start(f32[256,768]{1,0:T(8,128)} %copy-done.5) | copy-start | bytes 2359300
  246.2 28.6 %copy-start.40 = (f32[768]{0:T(1024)S(1)}, f32[768]{0:T(1024)}, u32[]{:S(2)}) copy-start(f32[768]{0:T(1024)} %copy-done.39) | copy-start | bytes 9220
  246.3 28.6 %copy-start.49 = (f32[256]{0:T(256)S(1)}, f32[256]{0:T(256)}, u32[]{:S(2)}) copy-start(f32[256]{0:T(256)} %copy-done.48) | copy-start | bytes 3076
  246.4 70.4 %copy-start.27 = (bf16[256,768]{1,0:T(8,128)(2,1)S(1)}, bf16[256,768]{1,0:T(8,128)(2,1)}, u32[]{:S(2)}) copy-start(bf16[256,768]{1,0:T(8,128)(2,1)} %param.33) | copy-start | bytes 1179652
  250.6 68.4 %copy-start.9 = (f32[256,768]{1,0:T(8,128)S(1)}, f32[256,768]{1,0:T(8,128)}, u32[]{:S(2)}) copy-start(f32[256,768]{1,0:T(8,128)} %get-tuple-element.27.o_ref) | copy-start | bytes 2359300
  250.6 197.3 %reduce-scatter.24.cloned.1.call-start = ((), (), s32[]{:S(2)}) async-start(), calls=%async_computation.19 | async-start | bytes 1548288 | tf_op jit(solution)/shard_map/reduce_scatter | solution.py:519
  318.9 22.5 %copy-start.4 = (f32[256,768]{1,0:T(8,128)}, f32[256,768]{1,0:T(8,128)S(1)}, u32[]{:S(2)}) copy-start(f32[256,768]{1,0:T(8,128)S(1)} %get-tuple-element.153) | copy-start | bytes 2359300
  320.9 137.6 %reduce-scatter.32.cloned.1.call-start = ((), (), s32[]{:S(2)}) async-start(), calls=%async_computation.23 | async-start | bytes 3932160 | tf_op jit(solution)/shard_map/reduce_scatter | solution.py:474
  328.3 177.0 %reduce-scatter.28.cloned.1.call-start = ((), (), s32[]{:S(2)}) async-start(), calls=%async_computation.21 | async-start | bytes 3932160 | tf_op jit(solution)/shard_map/reduce_scatter | solution.py:474
  337.3 216.0 %reduce-scatter.22.cloned.1.call-start = ((), (), s32[]{:S(2)}) async-start(), calls=%async_computation.18 | async-start | bytes 4202496 | tf_op jit(solution)/shard_map/reduce_scatter | solution.py:519
  363.8 40.2 %copy-start.8 = (f32[1536,768]{1,0:T(8,128)}, f32[1536,768]{1,0:T(8,128)S(1)}, u32[]{:S(2)}) copy-start(f32[1536,768]{1,0:T(8,128)S(1)} %get-tuple-element.152) | copy-start | bytes 14155780
  363.9 2.9 collective-permute-start.5
  367.1 36.9 %copy-start.7 = (f32[3,256,768]{2,1,0:T(8,128)}, f32[3,256,768]{2,1,0:T(8,128)S(1)}, u32[]{:S(2)}) copy-start(f32[3,256,768]{2,1,0:T(8,128)S(1)} %fusion.21) | copy-start | bytes 7077892
  367.1 14.8 %collective-permute-start.6 = (bf16[256,768]{1,0:T(8,128)(2,1)S(1)}, bf16[256,768]{1,0:T(8,128)(2,1)S(1)}, u32[]{:S(2)}, u32[]{:S(2)}) collective-permute-start(bf16[256,768]{1,0:T(8,128)(2,1)S(1)} %fusion.74), channel_id=1, source_target_pairs={{2,0},{3,1},{4,2},{5,3},{6,4},{7,5},{10,8},{11,9},{12,10},{13,11},... | collective-permute-start | bytes 1179656 | tf_op jit(solution)/shard_map/ppermute | solution.py:554
  368.4 15.1 %copy-start.60 = (bf16[1536,768]{1,0:T(8,128)(2,1)S(1)}, bf16[1536,768]{1,0:T(8,128)(2,1)}, u32[]{:S(2)}) copy-start(bf16[1536,768]{1,0:T(8,128)(2,1)} %get-tuple-element.29) | copy-start | bytes 7077892
  382.0 21.9 %collective-permute-start.7 = (bf16[256,768]{1,0:T(8,128)(2,1)S(1)}, bf16[256,768]{1,0:T(8,128)(2,1)S(1)}, u32[]{:S(2)}, u32[]{:S(2)}) collective-permute-start(bf16[256,768]{1,0:T(8,128)(2,1)S(1)} %fusion.50), channel_id=1, source_target_pairs={{2,0},{3,1},{4,2},{5,3},{6,4},{7,5},{10,8},{11,9},{12,10},{13,11},... | collective-permute-start | bytes 1179656 | tf_op jit(solution)/shard_map/ppermute | solution.py:554
  386.8 17.1 %copy-start.42 = (f32[768]{0:T(1024)S(1)}, f32[768]{0:T(1024)}, u32[]{:S(2)}) copy-start(f32[768]{0:T(1024)} %copy-done.41) | copy-start | bytes 9220
  413.9 184.4 %reduce-scatter.30.cloned.1.call-start = ((), (), s32[]{:S(2)}) async-start(), calls=%async_computation.22 | async-start | bytes 3932160 | tf_op jit(solution)/shard_map/reduce_scatter | solution.py:474
  422.7 14.4 %copy-start.13 = (bf16[256,768]{1,0:T(8,128)(2,1)S(1)}, bf16[256,768]{1,0:T(8,128)(2,1)}, u32[]{:S(2)}) copy-start(bf16[256,768]{1,0:T(8,128)(2,1)} %param.17) | copy-start | bytes 1179652
  422.8 22.6 %all-to-all-start.1 = ((bf16[8,24,512]{2,1,0:T(8,128)(2,1)}), bf16[8,24,512]{2,1,0:T(8,128)(2,1)S(1)}, u32[]{:S(2)}, u32[]{:S(2)}) async-start(bf16[8,24,512]{2,1,0:T(8,128)(2,1)} %bitcast.220), calls=%async_computation.5 | async-start | bytes 393216 | tf_op jit(solution)/shard_map/all_to_all | solution.py:494
  437.0 187.8 %reduce-scatter.36.cloned.1.call-start = ((), (), s32[]{:S(2)}) async-start(), calls=%async_computation.25 | async-start | bytes 215040
  447.9 204.2 %reduce-scatter.34.cloned.1.call-start = ((), (), s32[]{:S(2)}) async-start(), calls=%async_computation.24 | async-start | bytes 583680
  602.4 51.9 %copy-start.1 = (bf16[1,2048,768]{2,1,0:T(8,128)(2,1)S(1)}, bf16[1,2048,768]{2,1,0:T(8,128)(2,1)}, u32[]{:S(2)}) copy-start(bf16[1,2048,768]{2,1,0:T(8,128)(2,1)} %param.32) | copy-start | bytes 9437188
  (40 other events, 92.7 us)
Sparse Core Ops, SparseCore 0:
  11.4 67.5 all-gather.5
  80.6 36.5 all-gather.9
  119.4 46.0 all-gather.7
  234.9 39.8 reduce-scatter.19
  277.0 39.7 reduce-scatter.17
  319.6 25.5 reduce-scatter.37
  347.9 24.6 reduce-scatter.25
  375.5 36.6 reduce-scatter.23
  415.2 43.2 reduce-scatter.31
  461.4 43.8 reduce-scatter.27
  507.6 45.5 reduce-scatter.21
  556.1 42.2 reduce-scatter.29
  601.1 23.6 reduce-scatter.35
  627.5 24.5 reduce-scatter.33
